TPU v7x, 256 devices: a whole 4x4x8 slice. The times are simulated.
256 devices in a mesh: tm: 8 (over z), row: 8 (over x, core), obs: 4 (over y).
Axes of the slice: x: 4, y: 4, z: 8, core: 2. Of those that a mesh axis runs over, the one named last changes fastest.
Arguments:
- dyn_pattern: int32 [16, 8, 3], P('tm'), may hold values from 0 to 7
- dyn_values: float32 [16, 1024, 384], P('tm', ('row', 'obs')), may hold values from -0.3125 to 0.3125
- offsets: float32 [16, 1024], P('tm', ('row', 'obs')), may hold values from -6 to 6
- covariance: float32 [16, 1024, 1024], P('tm', ('row', 'obs')), may hold values from -1 to 14, as said below
- obs_block: int32 [16, 128], P('tm'), may hold values from 0 to 7
- obs_matrix: float32 [16, 128, 256], P('tm', 'obs'), may hold values from -0.375 to 0.375
- obs_data: float32 [16, 128], P('tm', 'obs'), may hold values from -6 to 6
Outputs:
- scan_dynamics: float32 [8, 1024, 1024], P('tm', ('row', 'obs'))
- scan_offset: float32 [8, 1024], P('tm', ('row', 'obs'))
- scan_covariance: float32 [8, 1024, 1024], P('tm', ('row', 'obs'))
- scan_factor: float32 [8, 1024, 512], P('tm', ('row', 'obs'))
- scan_information: float32 [8, 1024], P('tm', ('row', 'obs'))
Inputs may be any that keep to these rules, and one draw needn't show every extreme that they name: `dyn_pattern`: each entry names a block column. `obs_block`: each entry names a state block. Each covariance is symmetric and positive definite.
All inputs are finite; a program needn't handle non-finite values.
Results may differ from a plain program's by a relative error of at most 0.00019.
Values sent between devices are 32-bit elements; how exact they have to be, the bound alone decides.
A program may use at most 128 MiB of HBM per device.

v0:
```python
import jax
import jax.numpy as jnp
from jax import lax
from jax.sharding import PartitionSpec as P

largest_value = lax.Precision.HIGHEST


def shifted(block, axis, distance):
    devices = range(lax.axis_size(axis))
    route = [(i - distance, i) for i in devices if i - distance in devices]
    return lax.ppermute(block, axis, route)


def product(left, right):
    return jnp.dot(left, right, precision=largest_value, preferred_element_type=jnp.float32)


def lower_solve(lower, rhs):
    return lax.linalg.triangular_solve(lower, rhs, left_side=True, lower=True)


def assemble_dynamics(pattern, values):
    number_of_blocks = pattern.shape[0]
    per_row = pattern.shape[1]
    states = values.shape[0]
    block_extent = states // number_of_blocks
    indicator_matrix = (
        pattern[:, :, None] == jnp.arange(number_of_blocks, dtype=jnp.int32)[None, None, :]
    ).astype(jnp.float32)
    blocks = values.reshape(number_of_blocks, block_extent, per_row, block_extent)
    return jnp.einsum("ckd,cikj->cidj", indicator_matrix, blocks, precision=largest_value).reshape(
        states, states
    )


def assemble_factor(indices, matrix, number_of_blocks):
    item_count = matrix.shape[0]
    block_extent = matrix.shape[1] // 2
    reach = (indices[:, None] + jnp.arange(2, dtype=jnp.int32)[None, :]) % number_of_blocks
    indicator_matrix = (
        reach[:, :, None] == jnp.arange(number_of_blocks, dtype=jnp.int32)[None, None, :]
    ).astype(jnp.float32)
    piece_list = matrix.reshape(item_count, 2, block_extent)
    return jnp.einsum(
        "onr,onz->rzo", indicator_matrix, piece_list, precision=largest_value
    ).reshape(number_of_blocks * block_extent, item_count)


def combine(
    prior_dyn,
    prior_offsets,
    prior_cov,
    prior_factor,
    prior_zeta,
    own_dyn,
    own_offsets,
    own_cov,
    own_factor,
    own_zeta,
    row_start,
):
    panel_rows = prior_cov.shape[0]
    rank_width = own_factor.shape[1]
    own_pan = lax.dynamic_slice_in_dim(own_dyn, row_start, panel_rows, 0)
    gain_pan = product(prior_cov, own_factor)
    gain_rows = lax.all_gather(gain_pan, ("row", "obs"), axis=0, tiled=True)
    identity = jnp.eye(rank_width, dtype=jnp.float32)
    factor_pan = lax.dynamic_slice_in_dim(own_factor, row_start, panel_rows, 0)
    system = identity + lax.psum(product(factor_pan.T, gain_pan), ("row", "obs"))
    lower = jnp.linalg.cholesky(system)
    carried = product(own_dyn, gain_rows)
    observed = product(prior_dyn.T, own_factor)
    upper_part = lower_solve(lower, observed.T)
    weights = lower_solve(lower, carried.T).T
    weight_pan = lax.dynamic_slice_in_dim(weights, row_start, panel_rows, 0)
    spread_pan = product(prior_cov, own_dyn.T)
    moved = product(own_pan, lax.all_gather(spread_pan, ("row", "obs"), axis=0, tiled=True))
    new_dyn = product(own_pan, prior_dyn) - product(weight_pan, upper_part)
    new_cov = moved - product(weight_pan, weights.T) + own_cov
    residual = own_zeta - product(own_factor.T, prior_offsets)
    solved = lower_solve(lower, residual[:, None])[:, 0]
    new_offsets = product(own_pan, prior_offsets) + product(weight_pan, solved) + own_offsets
    upper_pan = lax.dynamic_slice_in_dim(upper_part, row_start, panel_rows, 1).T
    new_factor = jnp.concatenate([upper_pan, prior_factor], axis=1)
    new_zeta = jnp.concatenate([solved, prior_zeta])
    return (new_dyn, new_offsets, new_cov, new_factor, new_zeta)


def per_device(dyn_pattern, dyn_values, offsets, covariance, obs_block, obs_matrix, obs_data):
    panel_rows = covariance.shape[1]
    row_start = lax.axis_index(("row", "obs")) * panel_rows
    number_of_blocks = dyn_pattern.shape[1]
    obs_rows, obs_values = (
        lax.all_gather(obs_matrix, "obs", axis=1, tiled=True),
        lax.all_gather(obs_data, "obs", axis=1, tiled=True),
    )
    row_values, row_offsets = (
        lax.all_gather(dyn_values, ("row", "obs"), axis=1, tiled=True),
        lax.all_gather(offsets, ("row", "obs"), axis=1, tiled=True),
    )
    first_dyn = assemble_dynamics(dyn_pattern[0], row_values[0])
    second_dyn = assemble_dynamics(dyn_pattern[1], row_values[1])
    first_factor = assemble_factor(obs_block[0], obs_rows[0], number_of_blocks)
    second_factor = assemble_factor(obs_block[1], obs_rows[1], number_of_blocks)
    first_pan = lax.dynamic_slice_in_dim(first_factor, row_start, panel_rows, 0)
    dyn_pan, off_pan, cov_pan, fac_pan, zeta_full = combine(
        first_dyn,
        row_offsets[0],
        covariance[0],
        first_pan,
        obs_values[0],
        second_dyn,
        offsets[1],
        covariance[1],
        second_factor,
        obs_values[1],
        row_start,
    )
    later_pan, later_cov, later_off, later_fac, later_zeta = shifted(
        (dyn_pan, cov_pan, off_pan, fac_pan, zeta_full), "tm", -1
    )
    prior_full, later_full, later_factor, prior_offsets = (
        lax.all_gather(dyn_pan, ("row", "obs"), axis=0, tiled=True),
        lax.all_gather(later_pan, ("row", "obs"), axis=0, tiled=True),
        lax.all_gather(later_fac, ("row", "obs"), axis=0, tiled=True),
        lax.all_gather(off_pan, ("row", "obs"), axis=0, tiled=True),
    )
    top_dyn, top_off, top_cov, top_fac, top_zeta = combine(
        prior_full,
        prior_offsets,
        cov_pan,
        fac_pan,
        zeta_full,
        later_full,
        later_off,
        later_cov,
        later_factor,
        later_zeta,
        row_start,
    )
    even_turn = lax.axis_index("tm") % 2 == 0
    padded_fac = jnp.concatenate([fac_pan, jnp.zeros_like(fac_pan)], axis=1)
    padded_zeta = jnp.concatenate([zeta_full, jnp.zeros_like(zeta_full)])
    out_dyn = jnp.where(even_turn, top_dyn, dyn_pan)
    out_off = jnp.where(even_turn, top_off, off_pan)
    out_cov = jnp.where(even_turn, top_cov, cov_pan)
    out_fac = jnp.where(even_turn, top_fac, padded_fac)
    out_zeta = jnp.where(even_turn, top_zeta, padded_zeta)
    output_information = product(out_fac, out_zeta)
    return (out_dyn[None], out_off[None], out_cov[None], out_fac[None], output_information[None])


def solution(mesh):
    placed = (
        P("tm", None, None),
        P("tm", ("row", "obs"), None),
        P("tm", ("row", "obs")),
        P("tm", ("row", "obs"), None),
        P("tm", None),
        P("tm", "obs", None),
        P("tm", "obs"),
    )
    return jax.shard_map(
        per_device,
        mesh=mesh,
        in_specs=placed,
        out_specs=(
            P("tm", ("row", "obs"), None),
            P("tm", ("row", "obs")),
            P("tm", ("row", "obs"), None),
            P("tm", ("row", "obs"), None),
            P("tm", ("row", "obs")),
        ),
        check_vma=False,
    )
```

profile of v0, /device:TPU:1, one launch (start us, length us, event | category | flops | bytes accessed | tf_op | source)
XLA Modules:
  0.0 616.6 jit_solution(8064863237237655006)
XLA Ops:
  7.2 0.7 all-gather.10.cloned.1.call-update
  8.0 11.5 %all_gather.37 = f32[2,128,256]{2,1,0:T(8,128)S(1)} all-gather(f32[2,32,256]{2,1,0:T(8,128)} %param.16), channel_id=1, replica_groups=mesh['tm'=8,'row'=8,'obs'=4] {'obs'}, dimensions={1}, use_global_device_ids=true | all-gather | bytes 327680 | tf_op jit(solution)/shard_map/all_gather | solution.py:95
  19.5 0.8 slice_bitcast_fusion.12
  20.4 0.9 fusion.36
  21.4 1.5 fusion.42
  23.0 0.9 fusion.83
  24.0 40.9 %all-gather.10.cloned.1.call-done = f32[2,1024,384]{2,1,0:T(8,128)} async-done(((f32[2,32,384]{2,1,0:T(8,128)}), f32[2,1024,384]{2,1,0:T(8,128)}) %all-gather.10.cloned.1.call-update) | async-done | bytes 3145744 | tf_op jit(solution)/shard_map/all_gather | solution.py:99
  64.9 3.2 fusion.135
  68.2 3.6 reshape.312
  71.8 4.3 fusion.104
  76.1 2.0 copy-done
  78.1 4.9 convolution_bitcast_fusion.1
  83.7 0.9 convolution_bitcast_fusion
  84.9 88.9 %all-reduce.5.cloned.1.call-done = f32[128,128]{1,0:T(8,128)} async-done(((f32[128,128]{1,0:T(8,128)}), f32[128,128]{1,0:T(8,128)}) %all-reduce.5.cloned.1.call-update) | async-done | bytes 65552 | tf_op jit(solution)/shard_map/psum | solution.py:70
  173.8 0.9 convert_add_fusion.1
  174.8 0.9 fusion.77
  175.7 11.7 %cholesky.60 = f32[128,128]{1,0:T(8,128)S(1)} custom-call(f32[128,128]{1,0:T(8,128)S(1)} %fusion.77), custom_call_target="Cholesky" | custom-call | tf_op jit(solution)/shard_map/jit(cholesky)/cholesky | solution.py:71
  188.1 0.7 fusion.55
  188.7 9.8 %custom-call.31 = f32[1,128,128]{1,2,0:T(8,128)S(1)} custom-call(f32[1,128,128]{2,1,0:T(8,128)S(1)} %fusion.55), custom_call_target="InvertDiagBlocksLowerTriangular" | custom-call | tf_op jit(solution)/shard_map/triangular_solve/custom-call.4 | solution.py:20
  198.5 1.9 reshape.313
  200.4 4.3 fusion.107
  204.7 2.0 copy-done.2
  206.7 3.0 fusion
  210.5 1.3 collective-permute-start.1
  211.8 3.8 collective-permute-done.1
  216.3 42.2 %all_gather.38 = f32[1024,128]{1,0:T(8,128)S(1)} all-gather(f32[32,128]{1,0:T(8,128)S(1)} %bitcast.273), channel_id=1, replica_groups=mesh['tm'=8,'row'=8,'obs'=4] {'row','obs'}, dimensions={0}, use_global_device_ids=true | all-gather | bytes 540672 | tf_op jit(solution)/shard_map/all_gather | solution.py:67
  258.5 3.4 copy.79
  261.9 4.8 fusion.133
  267.8 3.0 fusion.6
  270.8 1.4 collective-permute-start
  272.3 4.8 collective-permute-done
  277.0 0.7 copy-done.12
  278.8 4.8 fusion.52
  284.1 1.9 fusion.138
  286.0 1.9 fusion.100
  288.0 0.7 all-gather.20.cloned.1.call-update
  288.7 40.4 %all-gather = f32[32,32,2]{1,2,0:T(2,128)S(1)} all-gather(f32[1,32,2]{1,2,0:T(2,128)S(1)} %bitcast.282), channel_id=1, replica_groups=mesh['tm'=8,'row'=8,'obs'=4] {'row','obs'}, dimensions={0}, use_global_device_ids=true | all-gather | bytes 8448 | tf_op jit(solution)/shard_map/all_gather | solution.py:100
  329.2 5.2 all-gather.1
  334.5 0.7 fusion.175
  335.8 6.7 %fusion.141 = f32[32,1024]{1,0:T(8,128)} fusion(f32[32,1024]{1,0:T(8,128)S(1)} %fusion.12, f32[1024,1024]{1,0:T(8,128)} %all-gather.12.cloned.1.call-done), kind=kOutput, calls=%fused_computation.205 | convolution fusion | flops 402653184 | bytes 4456448 | tf_op jit(solution)/shard_map/dot_general | solution.py:16
  344.0 1.3 collective-permute-start.2
  345.3 1.1 convolution_bitcast_fusion.9
  346.7 1.3 collective-permute-start.3
  348.3 63.1 %all-reduce.1 = f32[1024]{0:T(1024)S(1)} all-reduce(f32[1024]{0:T(1024)S(1)} %dynamic-update-slice.17), channel_id=1, replica_groups=mesh['tm'=8,'row'=8,'obs'=4] {'row','obs'}, use_global_device_ids=true, to_apply=%add.1 | all-reduce | flops 1024 | bytes 8192
  412.0 1.3 collective-permute-start.4
  413.4 5.8 fusion.140
  419.1 80.6 %all-reduce.7.cloned.1.call-done = f32[256,256]{0,1:T(8,128)} async-done(((f32[256,256]{0,1:T(8,128)}), f32[256,256]{0,1:T(8,128)}) %all-reduce.7.cloned.1.call-update) | async-done | bytes 262160 | tf_op jit(solution)/shard_map/psum | solution.py:70
  499.8 1.0 convert_add_fusion
  500.9 1.0 fusion.34
  501.9 11.7 %cholesky.115 = f32[128,128]{1,0:T(8,128)S(1)} custom-call(f32[128,128]{1,0:T(8,128)S(1)} %cholesky.141), custom_call_target="Cholesky" | custom-call | tf_op jit(solution)/shard_map/jit(cholesky)/cholesky | solution.py:71
  513.7 9.8 %custom-call.26 = f32[1,128,128]{1,2,0:T(8,128)S(1)} custom-call(f32[1,128,128]{2,1,0:T(8,128)S(1)} %get-tuple-element.62), custom_call_target="InvertDiagBlocksLowerTriangular" | custom-call | tf_op jit(solution)/shard_map/jit(cholesky)/cholesky | solution.py:71
  523.9 11.7 %cholesky.128 = f32[128,128]{1,0:T(8,128)S(1)} custom-call(f32[128,128]{1,0:T(8,128)S(1)} %convolution_subtract_fusion.3), custom_call_target="Cholesky" | custom-call | tf_op jit(solution)/shard_map/jit(cholesky)/cholesky | solution.py:71
  538.4 4.0 while.5
  539.0 1.4 bitcast_dynamic-update-slice_fusion.2
  541.0 1.4 bitcast_dynamic-update-slice_fusion.2
  542.4 19.9 %custom-call.33 = f32[2,128,128]{1,2,0:T(8,128)S(1)} custom-call(f32[2,128,128]{2,1,0:T(8,128)S(1)} %get-tuple-element.29), custom_call_target="InvertDiagBlocksLowerTriangular" | custom-call | tf_op jit(solution)/shard_map/triangular_solve/custom-call.5 | solution.py:20
  565.0 0.7 fusion.60
  566.4 9.2 %fusion.139 = f32[256,1024]{1,0:T(8,128)S(1)} fusion(f32[1024,256]{1,0:T(8,128)} %all-gather.20.cloned.1.call-done, f32[1024,1024]{1,0:T(8,128)} %all-gather.12.cloned.1.call-done), kind=kOutput, calls=%fused_computation.203 | convolution fusion | flops 3221225472 | bytes 6291456 | tf_op jit(solution)/shard_map/dot_general | solution.py:16
  577.6 0.7 fusion.24
  578.4 0.7 fusion.23
  579.1 4.1 fusion.14
  583.4 1.7 fusion.20
  585.0 19.4 %all-gather.22.cloned.1.call-done = f32[1024,1024]{1,0:T(8,128)} async-done(((f32[32,1024]{1,0:T(8,128)}), f32[1024,1024]{1,0:T(8,128)}) %all-gather.22.cloned.1.call-update) | async-done | bytes 4194320 | tf_op jit(solution)/shard_map/all_gather | solution.py:78
  604.4 5.4 fusion.11
  (127 shorter events, 18.0 us)
Async XLA Ops:
  7.2 16.8 %copy-start.15 = (s32[2,8,3]{1,0,2:T(2,128)S(1)}, s32[2,8,3]{1,0,2:T(2,128)}, u32[]{:S(2)}) copy-start(s32[2,8,3]{1,0,2:T(2,128)} %param.11) | copy-start | bytes 580
  7.2 57.8 %all-gather.10.cloned.1.call-start = ((), (), s32[]{:S(2)}) async-start(), calls=%async_computation | async-start | bytes 3244032 | tf_op jit(solution)/shard_map/all_gather | solution.py:99
  7.9 165.9 %all-reduce.5.cloned.1.call-start = ((), (), s32[]{:S(2)}) async-start(), calls=%async_computation.1 | async-start | bytes 131072 | tf_op jit(solution)/shard_map/psum | solution.py:70
  23.9 254.9 %all-gather.18.cloned.1.call-start = ((), (), s32[]{:S(2)}) async-start(), calls=%async_computation.5 | async-start | bytes 4325376 | tf_op jit(solution)/shard_map/all_gather | solution.py:78
  68.2 9.9 %copy-start.10 = (f32[2,32,1024]{2,1,0:T(8,128)S(1)}, f32[2,32,1024]{2,1,0:T(8,128)}, u32[]{:S(2)}) copy-start(f32[2,32,1024]{2,1,0:T(8,128)} %param.14) | copy-start | bytes 786436
  76.1 2.0 copy-start
  83.0 201.1 %all-gather.16.cloned.1.call-start = ((), (), s32[]{:S(2)}) async-start(), calls=%async_computation.4 | async-start | bytes 1081344 | tf_op jit(solution)/shard_map/all_gather | solution.py:126
  84.9 119.8 %copy-start.9 = (f32[8,128,128]{2,1,0:T(8,128)}, f32[8,128,128]{2,1,0:T(8,128)S(1)}, u32[]{:S(2)}) copy-start(f32[8,128,128]{2,1,0:T(8,128)S(1)} %copy.56) | copy-start | bytes 1572868
  204.7 2.0 copy-start.2
  210.5 5.1 collective-permute-start.1
  215.6 0.6 copy-start.13
  216.2 119.5 %all-gather.12.cloned.1.call-start = ((), (), s32[]{:S(2)}) async-start(), calls=%async_computation.2 | async-start | bytes 4325376 | tf_op jit(solution)/shard_map/all_gather | solution.py:125
  258.5 3.5 copy-start.1
  261.9 5.9 copy-start.6
  261.9 5.9 copy-start.3
  270.8 7.0 %copy-start.7 = (f32[32,1024]{1,0:T(8,128)}, f32[32,1024]{1,0:T(8,128)S(1)}, u32[]{:S(2)}) copy-start(f32[32,1024]{1,0:T(8,128)S(1)} %fusion.6) | copy-start | bytes 393220
  270.8 17.9 %copy-start.14 = (f32[2,32]{1,0:T(2,128)S(1)}, f32[2,32]{1,0:T(2,128)}, u32[]{:S(2)}) copy-start(f32[2,32]{1,0:T(2,128)} %param.13) | copy-start | bytes 772
  270.8 58.4 %copy-start.16 = (f32[2,32]{1,0:T(2,128)S(1)}, f32[2,32]{1,0:T(2,128)}, u32[]{:S(2)}) copy-start(f32[2,32]{1,0:T(2,128)} %param.17) | copy-start | bytes 772
  270.8 6.2 %collective-permute-start = (f32[32,1024]{1,0:T(8,128)S(1)}, f32[32,1024]{1,0:T(8,128)S(1)}, u32[]{:S(2)}, u32[]{:S(2)}) collective-permute-start(f32[32,1024]{1,0:T(8,128)S(1)} %fusion.6), channel_id=1, source_target_pairs={{32,0},{64,32},{96,64},{128,96},{160,128},{192,160},{224,192},{33,... | collective-permute-start | bytes 393224 | tf_op jit(solution)/shard_map/ppermute | solution.py:12
  277.0 0.7 copy-start.12
  277.7 135.6 %all-gather.14.cloned.1.call-start = ((), (), s32[]{:S(2)}) async-start(), calls=%async_computation.3 | async-start | bytes 4325376 | tf_op jit(solution)/shard_map/all_gather | solution.py:124
  278.3 221.5 %all-reduce.7.cloned.1.call-start = ((), (), s32[]{:S(2)}) async-start(), calls=%async_computation.6 | async-start | bytes 524288 | tf_op jit(solution)/shard_map/psum | solution.py:70
  283.5 59.0 %copy-start.17 = (u32[256]{0:T(256)S(1)}, u32[256]{0:T(256)}, u32[]{:S(2)}) copy-start(u32[256]{0:T(256)} %constant.217) | copy-start | bytes 3076
  284.1 127.4 %copy-start.5 = (f32[1024,256]{1,0:T(8,128)S(1)}, f32[1024,256]{1,0:T(8,128)}, u32[]{:S(2)}) copy-start(f32[1024,256]{1,0:T(8,128)} %all-gather.16.cloned.1.call-done) | copy-start | bytes 3145732
  286.0 2.0 copy-start.11
  287.9 278.5 %all-gather.20.cloned.1.call-start = ((), (), s32[]{:S(2)}) async-start(), calls=%async_computation.7 | async-start | bytes 1081344 | tf_op jit(solution)/shard_map/all_gather | solution.py:67
  288.6 315.7 %all-gather.22.cloned.1.call-start = ((), (), s32[]{:S(2)}) async-start(), calls=%async_computation.8 | async-start | bytes 4325376 | tf_op jit(solution)/shard_map/all_gather | solution.py:78
  344.0 68.1 %collective-permute-start.2 = (f32[256]{0:T(256)S(1)}, f32[256]{0:T(256)S(1)}, u32[]{:S(2)}, u32[]{:S(2)}) collective-permute-start(f32[256]{0:T(256)S(1)} %pad_maximum_fusion.5), channel_id=1, source_target_pairs={{32,0},{64,32},{96,64},{128,96},{160,128},{192,160},{224,192},{33,... | collective-permute-start | bytes 3080 | tf_op jit(solution)/shard_map/ppermute | solution.py:12
  346.7 236.7 %collective-permute-start.3 = (f32[32]{0:T(128)S(1)}, f32[32]{0:T(128)S(1)}, u32[]{:S(2)}, u32[]{:S(2)}) collective-permute-start(f32[32]{0:T(128)S(1)} %fusion.16), channel_id=1, source_target_pairs={{32,0},{64,32},{96,64},{128,96},{160,128},{192,160},{224,192},{33,... | collective-permute-start | bytes 392 | tf_op jit(solution)/shard_map/ppermute | solution.py:12
  412.0 173.0 %collective-permute-start.4 = (f32[32,1024]{1,0:T(8,128)S(1)}, f32[32,1024]{1,0:T(8,128)S(1)}, u32[]{:S(2)}, u32[]{:S(2)}) collective-permute-start(f32[32,1024]{1,0:T(8,128)S(1)} %fusion.12), channel_id=1, source_target_pairs={{32,0},{64,32},{96,64},{128,96},{160,128},{192,160},{224,192},{33,... | collective-permute-start | bytes 393224 | tf_op jit(solution)/shard_map/ppermute | solution.py:12
  575.6 3.5 copy-start.4
  575.6 3.5 copy-start.8
Sparse Core Ops, SparseCore 0:
  10.6 54.3 all-gather.9
  68.8 105.0 all-reduce.4
  177.3 50.6 all-gather.17
  231.3 47.2 all-gather.15
  281.3 50.4 all-gather.11
  335.2 50.5 all-gather.13
  389.3 110.4 all-reduce.6
  502.9 48.7 all-gather.19
  554.2 50.1 all-gather.21
where the time goes:
time: 624 us; the launch traced here: 617 us
  waiting for transfers between devices  240 us (38%)
  blocking collectives  162 us (26%)
  other arithmetic  82.1 us (13%)
  matrix products  81.7 us (13%)
  local copies, waits for them, and re-layouts  25.3 us (4%)
  between operations  16.8 us (3%)
  starting transfers between devices  7.9 us (1%)
    psum x2, waiting for transfers between devices, combine(): lax.psum(product(factor_pan.T, gain_pan), ('row', 'obs'))  170 us
    dot_general x25, matrix products, product(): jnp.dot(left, right, precision=largest_value, preferred_element_type=jnp....  65.1 us
    unnamed x1, blocking collectives  63.1 us
    another operation x10, other arithmetic, combine(): lower = jnp.linalg.cholesky(system)  47 us
    all_gather x1, blocking collectives, combine(): gain_rows = lax.all_gather(gain_pan, ('row', 'obs'), axis=0, tiled=True)  42.2 us
    all_gather x1, waiting for transfers between devices, per_device(): lax.all_gather(dyn_values, ('row', 'obs'), axis=1, tiled=True)  40.9 us
    all_gather x1, blocking collectives, per_device(): lax.all_gather(offsets, ('row', 'obs'), axis=1, tiled=True)  40.4 us
    another operation x8, other arithmetic, lower_solve(): return lax.linalg.triangular_solve(lower, rhs, left_side=True, lower=True)  30.5 us
  transfers between devices with their start and end apart: 14, of which 6 were waited for; matrix products, arithmetic and copies ran while one was open for 29% of the time, Pallas kernels for 0%

commit v1 on v0

v1 whole, which is shorter than its diff:
```python
import functools

import jax
import jax.numpy as jnp
from jax import lax
from jax.experimental import pallas as pl
from jax.experimental.pallas import tpu as pltpu
from jax.sharding import PartitionSpec as P

F32 = jnp.float32
BF = jnp.bfloat16
NN = (((1,), (0,)), ((), ()))
NT = (((1,), (1,)), ((), ()))
TN = (((0,), (0,)), ((), ()))
MESH = pl.DeviceIdType.MESH
VM = pl.BlockSpec(memory_space=pltpu.VMEM)
SM = pl.BlockSpec(memory_space=pltpu.SMEM)
ANY = pl.BlockSpec(memory_space=pl.ANY)
NB = 8
BW = 128
ST = NB * BW
GROUP = 32
SIDE = 4
TM_DEV = 8
PAN = 32


def halves(x):
    hi = x.astype(BF)
    return hi, (x - hi.astype(F32)).astype(BF)
def mm(a, b, dims):
    ah, al = a if isinstance(a, tuple) else halves(a)
    bh, bl = b if isinstance(b, tuple) else halves(b)
    d = functools.partial(lax.dot_general, dimension_numbers=dims, preferred_element_type=F32)
    return d(ah, bh) + (d(ah, bl) + d(al, bh))
def eye(n):
    rows = lax.broadcasted_iota(jnp.int32, (n, n), 0)
    cols = lax.broadcasted_iota(jnp.int32, (n, n), 1)
    return jnp.where(rows == cols, 1.0, 0.0).astype(F32)


def chol_inverse(s_ref, n_ref):
    n_ref[...] = eye(BW)
    sub = lax.broadcasted_iota(jnp.int32, (8, BW), 0)
    lane = lax.broadcasted_iota(jnp.int32, (32, BW), 1)

    def panel(b, carry):
        k0 = pl.multiple_of(b * 32, 32)
        r = [s_ref[pl.ds(k0 + 8 * t, 8), :] for t in range(4)]
        n = [n_ref[pl.ds(k0 + 8 * t, 8), :] for t in range(4)]
        a = [pltpu.roll(x, lax.rem(BW - k0, BW), 1) for x in r]
        for h in range(4):
            c = {t: [jnp.broadcast_to(a[t][:, 8 * h + j : 8 * h + j + 1], (8, BW)) for j in range(8)] for t in range(h, 4)}
            piv = jnp.ones((8, BW), F32)
            for j in range(8):
                p = jnp.broadcast_to(c[h][j][j : j + 1, :], (8, BW))
                inv = 1.0 / p
                piv = jnp.where(sub == j, p, piv)
                own = [c[h][m][j : j + 1, :] for m in range(8)]
                ra, rr, rn = a[h][j : j + 1, :], r[h][j : j + 1, :], n[h][j : j + 1, :]
                for t in range(h, 4):
                    f = c[t][j] * inv
                    if t == h:
                        f = jnp.where(sub > j, f, 0.0)
                    for m in range(j + 1, 8):
                        c[t][m] = c[t][m] - f * own[m]
                    if h < 3:
                        a[t] = a[t] - f * ra
                    r[t] = r[t] - f * rr
                    n[t] = n[t] - f * rn
            scale = lax.rsqrt(piv)
            scale = scale * (1.5 - 0.5 * piv * scale * scale)
            r[h] = r[h] * scale
            n[h] = n[h] * scale
        for t in range(4):
            n_ref[pl.ds(k0 + 8 * t, 8), :] = n[t]

        @pl.when(b < 3)
        def _():
            rows = jnp.concatenate(r, axis=0)
            later = jnp.where(lane >= k0 + 32, rows, 0.0)
            both = jnp.concatenate([rows, jnp.concatenate(n, axis=0)], axis=1)
            lh = later.astype(BF).astype(F32)
            bh = both.astype(BF).astype(F32)
            left = jnp.concatenate([lh, lh, later - lh], axis=0).astype(BF)
            right = jnp.concatenate([bh, both - bh, bh], axis=0).astype(BF)
            change = lax.dot_general(left, right, TN, preferred_element_type=F32)
            s_ref[...] = s_ref[...] - change[:, :BW]
            n_ref[...] = n_ref[...] - change[:, BW:]

        return carry

    lax.fori_loop(0, 4, panel, 0)

def chol_inverse_2(s_ref, linv_ref, t_ref, n_ref):
    t_ref[...] = s_ref[:BW, :BW]
    chol_inverse(t_ref, n_ref)
    n1 = n_ref[...]
    n1h = halves(n1)
    low = mm(s_ref[BW:, :BW], n1h, NT)
    lowh = halves(low)
    t_ref[...] = s_ref[BW:, BW:] - mm(lowh, lowh, NT)
    cross = mm(lowh, n1h, NN)
    chol_inverse(t_ref, n_ref)
    n2 = n_ref[...]
    linv_ref[:BW, :BW] = n1
    linv_ref[:BW, BW:] = jnp.zeros((BW, BW), F32)
    linv_ref[BW:, :BW] = -mm(n2, cross, NN)
    linv_ref[BW:, BW:] = n2


def times_dyn_t(x_ref, pat, rows, e):
    out = []
    for c in range(NB):
        xs = jnp.concatenate([x_ref[pat[e, c, k]] for k in range(3)], axis=1)
        out.append(mm(xs, rows(c), NT))
    return out


def dyn_times(z_ref, pat, rows, e, c):
    zs = jnp.concatenate([z_ref[pat[e, c, k]].reshape(BW, PAN) for k in range(3)], axis=0)
    return mm(rows(c), zs, NN)


def is_block(found, block):
    return (found == block).astype(F32)


def put_blocks(ref, x):
    for d in range(NB):
        ref[d] = x[:, d * BW : (d + 1) * BW]


def pack(y):
    return [
        jnp.concatenate([y[s * 8 : s * 8 + 8, q * PAN : q * PAN + PAN] for s in range(4)], axis=1)
        for q in range(GROUP)
    ]


def unpack(rec_ref, base, z_ref):
    for s in range(4):
        part = rec_ref[:, base : base + 8, s * PAN : s * PAN + PAN]
        z_ref[:, :, s * 8 : s * 8 + 8, :] = part.reshape(NB, 4, 8, PAN)


def factor_rows(blk, mat):
    at = jnp.broadcast_to(blk.astype(F32), (BW, BW)).T
    out = []
    for d in range(NB):
        before = (d + NB - 1) % NB
        out.append(jnp.where(at == d, mat[:, :BW], 0.0) + jnp.where(at == before, mat[:, BW:], 0.0))
    return out


class Gather:
    def __init__(self, place, src, buf, send, recv, swapped):
        tm, row, obs = place
        x, core = row // 2, lax.rem(row, 2)
        self.core, self.buf, self.src = core, buf, src
        self.i, self.j = (obs, x) if swapped else (x, obs)
        self.send, self.recv = send, recv

        def device(i, j, c):
            xx, yy = (j, i) if swapped else (i, j)
            return (tm, 2 * xx + c, yy)

        self.device = device

    def copy(self, src, dst, n, device):
        return pltpu.make_async_remote_copy(
            src_ref=src, dst_ref=dst, send_sem=self.send.at[n], recv_sem=self.recv.at[n],
            device_id=device, device_id_type=MESH,
        )

    def first(self, d):
        piece = self.buf.at[self.core, self.i, self.j]
        j = lax.rem(self.j + d, SIDE)
        return self.copy(self.src if self.src is not None else piece, piece, d - 1, self.device(self.i, j, self.core))

    def second(self, d):
        block = self.buf.at[self.core, self.i]
        i = lax.rem(self.i + d, SIDE)
        return self.copy(block, block, 2 + d, self.device(i, self.j, self.core))

    def across(self, d):
        block = self.buf.at[self.core, lax.rem(self.i + SIDE - d, SIDE)]
        return self.copy(block, block, 6 + d, self.device(self.i, self.j, 1 - self.core))

    def phase1(self):
        for d in range(1, SIDE):
            self.first(d).start()

    def phase2(self):
        for d in range(1, SIDE):
            self.first(d).wait_recv()
        for d in range(1, SIDE):
            self.second(d).start()
        self.across(0).start()

    def phase3(self):
        for d in range(1, SIDE):
            self.second(d).wait_recv()
            self.across(d).start()

    def finish(self):
        for d in range(SIDE):
            self.across(d).wait_recv()

    def drain(self):
        for d in range(1, SIDE):
            self.first(d).wait_send()
            self.second(d).wait_send()
        for d in range(SIDE):
            self.across(d).wait_send()


class Swap:
    def __init__(self, place, src, dst, send, recv, own):
        self.tm, row, obs = place
        self.me = row * SIDE + obs
        self.src, self.dst, self.send, self.recv, self.own = src, dst, send, recv, own

    def copy(self, off):
        t = lax.rem(self.me + off, GROUP)
        return pltpu.make_async_remote_copy(
            src_ref=self.src.at[t], dst_ref=self.dst.at[self.me],
            send_sem=self.send.at[off], recv_sem=self.recv.at[off],
            device_id=(self.tm, t // SIDE, lax.rem(t, SIDE)), device_id_type=MESH,
        )

    def mine(self):
        return pltpu.make_async_copy(self.src.at[self.me], self.dst.at[self.me], self.own)

    def start(self):
        def begin(off, carry):
            self.copy(off).start()
            return carry

        lax.fori_loop(1, GROUP, begin, 0)
        self.mine().start()

    def finish(self):
        def end(off, carry):
            self.copy(off).wait_recv()
            return carry

        self.mine().wait()
        lax.fori_loop(1, GROUP, end, 0)

    def drain(self):
        def end(off, carry):
            self.copy(off).wait_send()
            return carry

        lax.fori_loop(1, GROUP, end, 0)


def kernel(
    pat, vals, offs, cov, blk, omat, odat,
    out_dyn, out_off, out_cov, out_fac, out_info,
    cov_v, obs_v, vi, vj, ga, gb, phi, s1, t1, n1, linv_v, s2, linv2_v,
    g_v, k_v, u_v, o_v, xt, pk, rec, lamt, lamt_a, bz, ba, c_pan, ca, g2a, g2b, g2_v, k2_v,
    pk2, rec2, fac2, c2, lam2, vec, vec_in, lam, fac, z1, z2, kb_v,
    obs_s, obs_r, gat_s, gat_r, swap_s, swap_r, z_s, z_r, own,
):
    tm, row, obs = lax.axis_index("tm"), lax.axis_index("row"), lax.axis_index("obs")
    place = (tm, row, obs)
    x, core = row // 2, lax.rem(row, 2)
    me = row * SIDE + obs
    row0 = pl.multiple_of(me * PAN, PAN)
    lo = pl.multiple_of(obs * PAN, PAN)
    odd = lax.rem(tm, 2) == 1
    up = (lax.rem(tm + 1, TM_DEV), row, obs)
    down = (lax.rem(tm + TM_DEV - 1, TM_DEV), row, obs)

    def rows_i(c):
        return vi[c % 2, c // 2].reshape(BW, 3 * BW)

    def rows_j(c):
        return vj[c % 2, :, c // 2].reshape(BW, 3 * BW)

    def obs_copy(e, d):
        return pltpu.make_async_remote_copy(
            src_ref=omat.at[e], dst_ref=obs_v.at[e, obs], send_sem=obs_s.at[e, d - 1], recv_sem=obs_r.at[e, d - 1],
            device_id=(tm, row, lax.rem(obs + d, SIDE)), device_id_type=MESH,
        )

    def z_copy(n, src, dst, device):
        return pltpu.make_async_remote_copy(
            src_ref=src, dst_ref=dst, send_sem=z_s.at[n], recv_sem=z_r.at[n], device_id=device, device_id_type=MESH
        )

    gather_i = Gather(place, vals.at[0], vi, gat_s.at[0], gat_r.at[0], False)
    gather_j = Gather(place, vals.at[1], vj, gat_s.at[1], gat_r.at[1], True)
    gather_ga = Gather(place, None, ga, gat_s.at[2], gat_r.at[2], False)
    gather_gb = Gather(place, None, gb, gat_s.at[3], gat_r.at[3], True)
    gather_2a = Gather(place, None, g2a, gat_s.at[4], gat_r.at[4], False)
    gather_2b = Gather(place, None, g2b, gat_s.at[5], gat_r.at[5], True)
    swap1 = Swap(place, pk, rec, swap_s.at[0], swap_r.at[0], own.at[4])
    swap2 = Swap(place, pk2, rec2, swap_s.at[1], swap_r.at[1], own.at[5])
    up_lam = z_copy(0, lamt, lamt_a, up)
    up_b = z_copy(1, bz, ba, up)
    up_cov = z_copy(2, c_pan, ca, up)
    down_dyn = z_copy(3, lam2, out_dyn.at[0], down)
    down_cov = z_copy(4, c2, out_cov.at[0], down)
    down_fac = z_copy(5, fac2, out_fac.at[0, :, 0 : 2 * BW], down)
    down_vec = z_copy(6, vec, vec_in, down)

    local_cov = pltpu.make_async_copy(cov, cov_v, own.at[0])
    local_i = pltpu.make_async_copy(vals.at[0], vi.at[core, x, obs], own.at[1])
    local_j = pltpu.make_async_copy(vals.at[1], vj.at[core, obs, x], own.at[2])
    local_obs = pltpu.make_async_copy(omat, obs_v.at[:, obs], own.at[3])
    local_obs.start()
    local_cov.start()
    local_i.start()
    local_j.start()

    barrier = pltpu.get_barrier_semaphore()

    def greet(off, carry):
        t = lax.rem(me + off, GROUP)
        pl.semaphore_signal(barrier, inc=1, device_id=(tm, t // SIDE, lax.rem(t, SIDE)), device_id_type=MESH)
        return carry

    lax.fori_loop(1, GROUP, greet, 0)
    pl.semaphore_signal(barrier, inc=1, device_id=up, device_id_type=MESH)
    pl.semaphore_signal(barrier, inc=1, device_id=down, device_id_type=MESH)
    pl.semaphore_wait(barrier, GROUP + 1)

    for d in range(1, SIDE):
        obs_copy(1, d).start()
    for d in range(1, SIDE):
        obs_copy(0, d).start()
    gather_i.phase1()
    gather_j.phase1()

    local_obs.wait()
    for d in range(1, SIDE):
        obs_copy(1, d).wait_recv()
    for d, part in enumerate(factor_rows(blk[1:2, :], obs_v[1].reshape(BW, 2 * BW))):
        phi[1, :, d * BW : (d + 1) * BW] = part
    local_cov.wait()
    gain = mm(cov_v[0], phi[1], NT)
    ga[core, x, obs] = gain[0:16]
    small = jnp.concatenate([offs[...], odat[...]], axis=0)
    gb[core, obs, x, 0:16] = gain[16:32]
    gb[core, obs, x, 16:24] = jnp.zeros((8, BW), F32)
    gb[core, obs, x, 16:20, 0:PAN] = small
    gather_ga.phase1()
    gather_gb.phase1()
    gather_ga.phase2()
    gather_gb.phase2()
    local_i.wait()
    local_j.wait()
    gather_i.phase2()
    gather_j.phase2()
    gather_ga.phase3()
    gather_gb.phase3()
    for d in range(1, SIDE):
        obs_copy(0, d).wait_recv()
    for d, part in enumerate(factor_rows(blk[0:1, :], obs_v[0].reshape(BW, 2 * BW))):
        phi[0, :, d * BW : (d + 1) * BW] = part
    gather_ga.finish()
    gather_gb.finish()

    vecs = []
    for c in range(NB):
        both = jnp.concatenate([ga[c % 2, c // 2], gb[c % 2, :, c // 2, 0:16]], axis=1)
        g_v[c * BW : (c + 1) * BW, :] = both.reshape(BW, BW)
        vecs.append(jnp.concatenate([gb[c % 2, o, c // 2, 16:24, 0:PAN] for o in range(SIDE)], axis=1))
    zeta_i = jnp.broadcast_to(vecs[0][2:3, :], (8, BW))
    zeta_j = jnp.broadcast_to(vecs[0][3:4, :], (8, BW))
    b_i = jnp.concatenate([jnp.broadcast_to(v[0:1, :], (8, BW)) for v in vecs], axis=1)
    b_j = jnp.concatenate([jnp.broadcast_to(v[1:2, :], (8, BW)) for v in vecs], axis=1)
    g = halves(g_v[...])
    phi_j = halves(phi[1])
    s1[...] = eye(BW) + mm(phi_j, g, NN)
    chol_inverse(s1, linv_v)
    linv = halves(linv_v[...])
    k = mm(g, linv, NT)
    k_v[...] = k
    for c in range(NB):
        kb_v[c] = k[c * BW : (c + 1) * BW, :]
    kh = halves(k)
    p = cov_v[0] - mm(k_v[pl.ds(row0, PAN), :], kh, NT)
    solved = mm(zeta_j - mm(b_i, phi_j, NT), linv, NT)
    xrow = b_i + mm(solved, kh, NT)
    gather_i.phase3()
    gather_j.phase3()
    gather_i.finish()

    for c in range(NB):
        t = mm(phi[1, :, c * BW : (c + 1) * BW], rows_i(c), NN)
        for d in range(NB):
            part = jnp.zeros((BW, BW), F32) if c == 0 else o_v[d]
            for n in range(3):
                part = part + is_block(pat[0, c, n], d) * t[:, n * BW : (n + 1) * BW]
            o_v[d] = part
    for d in range(NB):
        u_v[d] = mm(linv, o_v[d], NN)
    t1[...] = u_v[row].T
    upper = t1[pl.ds(lo, PAN), :]
    drop = mm(upper, kh, NT)
    for c in range(NB):
        rows = rows_i(c)
        w = jnp.zeros((BW, BW), F32)
        for n in range(3):
            w = w + is_block(pat[0, c, n], row) * rows[:, n * BW : (n + 1) * BW]
        t1[...] = w.T
        sl = slice(c * BW, (c + 1) * BW)
        xt[c] = jnp.concatenate([p[:, sl], t1[pl.ds(lo, PAN), :] - drop[:, sl], xrow[:, sl]], axis=0)
    gather_j.finish()
    y = jnp.concatenate(times_dyn_t(xt, pat, rows_j, 1), axis=1)
    for q, part in enumerate(pack(y[:PAN, :])):
        pk[q] = part
    swap1.start()
    lamt[...] = y[PAN : 2 * PAN, :]
    b_own = y[2 * PAN :, :] + b_j
    bz[...] = b_own

    @pl.when(jnp.logical_not(odd))
    def _():
        up_lam.start()
        up_b.start()

    for d in range(NB):
        o_v[d] = phi[0, :, d * BW : (d + 1) * BW]
    t1[...] = o_v[row].T
    prior = t1[pl.ds(lo, PAN), :]
    fac[:, :BW] = upper
    fac[:, BW : 2 * BW] = prior
    fac[:, 2 * BW :] = jnp.zeros((PAN, 2 * BW), F32)
    info = mm(solved, upper, NT) + mm(zeta_i, prior, NT)
    swap1.finish()

    unpack(rec, 0, z1)
    for c in range(NB):
        sl = slice(c * BW, (c + 1) * BW)
        c_pan[:, sl] = dyn_times(z1, pat, rows_j, 1, c).T + cov_v[1, :, sl]

    def my_panel(full):
        put_blocks(o_v.at[:, 0:8, :], full)
        block = o_v[row, 0:8, :]
        return pltpu.roll(block, lax.rem(BW - lo, BW), 1)[0:1, 0:PAN]

    @pl.when(jnp.logical_not(odd))
    def _():
        up_cov.start()
        pieces = pltpu.make_async_copy(fac.at[:, 0 : 2 * BW], out_fac.at[0, :, 2 * BW :], own.at[6])
        pieces.start()
        pieces.wait()
        down_vec.wait_recv()
        out_off[...] = vec_in[0:1, 0:PAN]
        out_info[...] = info[0:1, :] + vec_in[1:2, 0:PAN]
        down_dyn.wait_recv()
        down_cov.wait_recv()
        down_fac.wait_recv()
        up_lam.wait_send()
        up_b.wait_send()
        up_cov.wait_send()

    @pl.when(odd)
    def _():
        out_off[...] = my_panel(b_own)
        out_info[...] = info[0:1, :]
        ones = [
            pltpu.make_async_copy(c_pan, out_cov.at[0], own.at[6]),
            pltpu.make_async_copy(fac, out_fac.at[0], own.at[7]),
        ]
        for one in ones:
            one.start()
        up_lam.wait_recv()
        up_b.wait_recv()
        lam_parts = [jnp.zeros((PAN, BW), F32) for _ in range(NB)]
        ak = jnp.zeros((PAN, BW), F32)
        for n in range(3):
            b = pat[1, row, n]
            block = vj[core, obs, x, :, n * BW : (n + 1) * BW]
            mine = halves(block)
            t = mm(mine, vi[lax.rem(b, 2), lax.div(b, 2)].reshape(BW, 3 * BW), NN)
            for m in range(3):
                at = pat[0, b, m]
                for d in range(NB):
                    lam_parts[d] = lam_parts[d] + is_block(at, d) * t[:, m * BW : (m + 1) * BW]
            ak = ak + mm(mine, kb_v[b], NN)
        akh = halves(ak)
        for d in range(NB):
            lam[:, d * BW : (d + 1) * BW] = lam_parts[d] - mm(akh, u_v[d], NN)
        dyn_out = pltpu.make_async_copy(lam, out_dyn.at[0], own.at[8])
        dyn_out.start()

        up_cov.wait_recv()
        u = jnp.concatenate([u_v[d] for d in range(NB)], axis=1)
        phi_b = halves(jnp.concatenate([u, phi[0]], axis=0))
        gain2 = mm(ca[...], phi_b, NT)
        g2a[core, x, obs] = gain2[:, :BW]
        g2b[core, obs, x] = gain2[:, BW:]
        gather_2a.phase1()
        gather_2b.phase1()
        gather_2a.phase2()
        gather_2b.phase2()
        gather_2a.phase3()
        gather_2b.phase3()
        gather_2a.finish()
        gather_2b.finish()
        for c in range(NB):
            g2_v[c * BW : (c + 1) * BW, :BW] = g2a[c % 2, c // 2].reshape(BW, BW)
            g2_v[c * BW : (c + 1) * BW, BW:] = g2b[c % 2, :, c // 2].reshape(BW, BW)
        g2 = halves(g2_v[...])
        s2[...] = eye(2 * BW) + mm(phi_b, g2, NN)
        chol_inverse_2(s2, linv2_v, t1, n1)
        linv2 = halves(linv2_v[...])
        k2 = mm(g2, linv2, NT)
        k2_v[...] = k2
        k2h = halves(k2)
        p2 = ca[...] - mm(k2_v[pl.ds(row0, PAN), :], k2h, NT)
        la = lamt_a[...]
        upper2 = mm(mm(la, phi_b, NT), linv2, NT)
        fac2[...] = upper2
        down_fac.start()
        mt = la - mm(upper2, k2h, NT)
        zeta = jnp.concatenate([solved, zeta_i], axis=1)
        bp = ba[...]
        solved2 = mm(zeta - mm(bp, phi_b, NT), linv2, NT)
        xs = jnp.concatenate([p2, mt, bp + mm(solved2, k2h, NT)], axis=0)
        put_blocks(xt, xs)
        h = jnp.concatenate(times_dyn_t(xt, pat, rows_i, 0), axis=1)
        put_blocks(xt, h - mm(mm(xs, u, NT), k_v[...], NT))
        y2 = jnp.concatenate(times_dyn_t(xt, pat, rows_j, 1), axis=1)
        for q, part in enumerate(pack(y2[:PAN, :])):
            pk2[q, 0:8] = part
        for q, part in enumerate(pack(y2[PAN : 2 * PAN, :])):
            pk2[q, 8:16] = part
        swap2.start()
        vec[...] = jnp.zeros((8, BW), F32)
        vec[0:1, 0:PAN] = my_panel(y2[2 * PAN :, :] + b_own)
        vec[1:2, 0:PAN] = mm(solved2, upper2, NT)[0:1, :]
        down_vec.start()
        swap2.finish()
        unpack(rec2, 8, z1)
        for c in range(NB):
            lam2[:, c * BW : (c + 1) * BW] = z1[c].reshape(BW, PAN).T
        down_dyn.start()
        unpack(rec2, 0, z1)
        uz = jnp.zeros((BW, PAN), F32)
        for d in range(NB):
            uz = uz + mm(u_v[d], z1[d].reshape(BW, PAN), NN)
        kz = mm(k_v[...], uz, NN)
        for c in range(NB):
            part = dyn_times(z1, pat, rows_i, 0, c) - kz[c * BW : (c + 1) * BW, :]
            z2[c] = part.reshape(4, PAN, PAN)
        for c in range(NB):
            sl = slice(c * BW, (c + 1) * BW)
            c2[:, sl] = dyn_times(z2, pat, rows_j, 1, c).T + c_pan[:, sl]
        down_cov.start()
        for one in ones:
            one.wait()
        dyn_out.wait()
        gather_2a.drain()
        gather_2b.drain()
        swap2.drain()
        for one in (down_fac, down_vec, down_dyn, down_cov):
            one.wait_send()

    for e in range(2):
        for d in range(1, SIDE):
            obs_copy(e, d).wait_send()
    for one in (gather_i, gather_j, gather_ga, gather_gb):
        one.drain()
    swap1.drain()


def vmem(*shape):
    return pltpu.VMEM(shape, F32)


def dma(*shape):
    return pltpu.SemaphoreType.DMA(shape)


SCRATCH = [
    vmem(2, PAN, ST), vmem(2, SIDE, PAN, 2 * BW),
    vmem(2, SIDE, SIDE, PAN, 3 * BW), vmem(2, SIDE, SIDE, PAN, 3 * BW),
    vmem(2, SIDE, SIDE, 16, BW), vmem(2, SIDE, SIDE, 24, BW),
    vmem(2, BW, ST),
    vmem(BW, BW), vmem(BW, BW), vmem(BW, BW), vmem(BW, BW),
    vmem(2 * BW, 2 * BW), vmem(2 * BW, 2 * BW),
    vmem(ST, BW), vmem(ST, BW), vmem(NB, BW, BW), vmem(NB, BW, BW), vmem(NB, 2 * PAN + 8, BW),
    vmem(GROUP, 8, BW), vmem(GROUP, 8, BW),
    vmem(PAN, ST), vmem(PAN, ST), vmem(8, ST), vmem(8, ST), vmem(PAN, ST), vmem(PAN, ST),
    vmem(2, SIDE, SIDE, PAN, BW), vmem(2, SIDE, SIDE, PAN, BW),
    vmem(ST, 2 * BW), vmem(ST, 2 * BW),
    vmem(GROUP, 16, BW), vmem(GROUP, 16, BW),
    vmem(PAN, 2 * BW), vmem(PAN, ST), vmem(PAN, ST), vmem(8, BW), vmem(8, BW),
    vmem(PAN, ST), vmem(PAN, 4 * BW),
    vmem(NB, 4, PAN, PAN), vmem(NB, 4, PAN, PAN), vmem(NB, BW, BW),
    dma(2, 3), dma(2, 3), dma(6, 10), dma(6, 10), dma(2, GROUP), dma(2, GROUP), dma(7), dma(7), dma(9),
]


def per_device(*args):
    outs = [(1, PAN, ST), (1, PAN), (1, PAN, ST), (1, PAN, 4 * BW), (1, PAN)]
    return pl.pallas_call(
        kernel,
        out_shape=[jax.ShapeDtypeStruct(s, F32) for s in outs],
        in_specs=[SM, ANY, VM, ANY, VM, ANY, VM],
        out_specs=[ANY, VM, ANY, ANY, VM],
        scratch_shapes=SCRATCH,
        compiler_params=pltpu.CompilerParams(
            collective_id=0, has_side_effects=True, vmem_limit_bytes=50 << 20
        ),
    )(*args)


def solution(mesh):
    placed = (
        P("tm", None, None),
        P("tm", ("row", "obs"), None),
        P("tm", ("row", "obs")),
        P("tm", ("row", "obs"), None),
        P("tm", None),
        P("tm", "obs", None),
        P("tm", "obs"),
    )
    return jax.shard_map(
        per_device,
        mesh=mesh,
        in_specs=placed,
        out_specs=(
            P("tm", ("row", "obs"), None),
            P("tm", ("row", "obs")),
            P("tm", ("row", "obs"), None),
            P("tm", ("row", "obs"), None),
            P("tm", ("row", "obs")),
        ),
        check_vma=False,
    )
```

time: 624 us -> 100 us (0.16); the launches traced: 617 us -> 99.7 us
  waiting for transfers between devices: 240 us -> 0 us
  blocking collectives: 162 us -> 0 us
  Pallas kernels: 0 us -> 92.6 us
  other arithmetic: 82.1 us -> 0 us
  matrix products: 81.7 us -> 0 us
  local copies, waits for them, and re-layouts: 25.3 us -> 6.43 us
  between operations: 16.8 us -> 0.68 us
  starting transfers between devices: 7.9 us -> 0 us
    psum x2 -> x0, waiting for transfers between devices: 170 us -> none  [combine(): lax.psum(product(factor_pan.T, gain_pan), ('row', 'obs'))]
    all_gather x4 -> x0, blocking collectives: 99.3 us -> none  [the longest x1 42.2 us: combine(): gain_rows = lax.all_gather(gain_pan, ('row', 'obs'), axis=0, tiled=True)]
    pallas_call x0 -> x1, Pallas kernels: none -> 92.6 us  [per_device(): pl.pallas_call(kernel, out_shape=[jax.ShapeDtypeStruct(s, F32) for s in o...]
    another operation x18 -> x0, other arithmetic: 77.5 us -> none  [the longest x10 47 us: combine(): lower = jnp.linalg.cholesky(system)]
    dot_general x29 -> x0, matrix products: 75.5 us -> none  [the longest x25 65.1 us: product(): jnp.dot(left, right, precision=largest_value, preferred_element_type=jnp....]
    unnamed x1 -> x0, blocking collectives: 63.1 us -> none
    all_gather x7 -> x0, waiting for transfers between devices: 60.3 us -> none  [the longest x1 40.9 us: per_device(): lax.all_gather(dyn_values, ('row', 'obs'), axis=1, tiled=True)]
    another operation x13 -> x0, local copies, waits for them, and re-layouts: 9.71 us -> none  [the longest x2 5.52 us: assemble_dynamics(): values.reshape(number_of_blocks, block_extent, per_row, block_extent)]
  transfers between devices with their start and end apart: 14 -> 0, of which waited for: 6 -> 0; matrix products, arithmetic and copies ran while one was open for 29% -> 0% of each run, Pallas kernels for 0% -> 0%
where the time goes in v1:
time: 100 us; the launch traced here: 99.7 us
  Pallas kernels  92.6 us (93%)
  local copies, waits for them, and re-layouts  6.43 us (6%)
    pallas_call x1, Pallas kernels, per_device(): pl.pallas_call(kernel, out_shape=[jax.ShapeDtypeStruct(s, F32) for s in o...  92.6 us
    unnamed x18, local copies, waits for them, and re-layouts  6.43 us

profile of v1, /device:TPU:1, one launch (start us, length us, event | category | flops | bytes accessed | tf_op | source)
XLA Modules:
  0.0 99.7 jit_solution(1216446253792816185)
XLA Ops:
  0.6 0.0 copy-start.5
  0.6 0.0 copy-start.4
  0.7 0.0 copy-start.3
  0.7 0.8 copy.12.pat
  1.4 0.0 copy-done.5
  1.4 0.0 copy-done.4
  1.4 0.0 copy-done.3
  1.5 0.0 copy-start
  1.5 0.9 copy-done
  2.4 0.0 copy-start.1
  2.4 0.9 copy-done.1
  3.3 0.0 copy-start.2
  3.3 0.8 copy-done.2
  4.1 92.6 %shard_map.110 = (f32[1,32,1024]{2,1,0:T(8,128)S(1)}, f32[1,32]{1,0:T(1,128)S(1)}, f32[1,32,1024]{2,1,0:T(8,128)S(1)}, f32[1,32,512]{2,1,0:T(8,128)S(1)}, f32[1,32]{1,0:T(1,128)S(1)}) custom-call(s32[2,8,3]{2,1,0:T(8,128)S(1)} %copy.12.pat, f32[2,32,384]{2,1,0:T(8,128)S(1)} %copy-done.1, f32[2,32]{1,0:T(2,128)S(1)} %copy-done.3, f32[2,32,1024]{2,1,0:T(8,128)S(1)} %copy-done, ...), custom_call_target="tpu_custom_call" | custom-call | tf_op jit(solution)/shard_map/pallas_call | solution.py:604
  96.8 0.7 copy.18
  97.4 0.5 copy.19
  97.9 0.7 copy.20
  98.6 0.6 copy.21
  99.2 0.5 copy.22
Async XLA Ops:
  0.6 0.8 copy-start.5
  0.6 0.8 copy-start.4
  0.7 0.8 copy-start.3
  1.5 1.0 copy-start
  2.4 0.9 copy-start.1
  3.3 0.8 copy-start.2

commit v2 on v1

--- a/solution.py
+++ b/solution.py
@@ -23,6 +23,7 @@
 SIDE = 4
 TM_DEV = 8
 PAN = 32
+CHUNK = 256
 
 
 def halves(x):
@@ -112,13 +113,13 @@
 def times_dyn_t(x_ref, pat, rows, e):
     out = []
     for c in range(NB):
-        xs = jnp.concatenate([x_ref[pat[e, c, k]] for k in range(3)], axis=1)
+        xs = jnp.concatenate([x_ref[pat[k, e, c]] for k in range(3)], axis=1)
         out.append(mm(xs, rows(c), NT))
     return out
 
 
 def dyn_times(z_ref, pat, rows, e, c):
-    zs = jnp.concatenate([z_ref[pat[e, c, k]].reshape(BW, PAN) for k in range(3)], axis=0)
+    zs = jnp.concatenate([z_ref[pat[k, e, c]].reshape(BW, PAN) for k in range(3)], axis=0)
     return mm(rows(c), zs, NN)
 
 
@@ -138,9 +139,9 @@
     ]
 
 
-def unpack(rec_ref, base, z_ref):
+def unpack(rec_ref, z_ref):
     for s in range(4):
-        part = rec_ref[:, base : base + 8, s * PAN : s * PAN + PAN]
+        part = rec_ref[:, :, s * PAN : s * PAN + PAN]
         z_ref[:, :, s * 8 : s * 8 + 8, :] = part.reshape(NB, 4, 8, PAN)
 
 
@@ -220,6 +221,7 @@
         self.tm, row, obs = place
         self.me = row * SIDE + obs
         self.src, self.dst, self.send, self.recv, self.own = src, dst, send, recv, own
+        self.low = 0 if own is None else 1
 
     def copy(self, off):
         t = lax.rem(self.me + off, GROUP)
@@ -237,31 +239,33 @@
             self.copy(off).start()
             return carry
 
-        lax.fori_loop(1, GROUP, begin, 0)
-        self.mine().start()
+        lax.fori_loop(self.low, GROUP, begin, 0)
+        if self.low:
+            self.mine().start()
 
     def finish(self):
         def end(off, carry):
             self.copy(off).wait_recv()
             return carry
 
-        self.mine().wait()
-        lax.fori_loop(1, GROUP, end, 0)
+        if self.low:
+            self.mine().wait()
+        lax.fori_loop(self.low, GROUP, end, 0)
 
     def drain(self):
         def end(off, carry):
             self.copy(off).wait_send()
             return carry
 
-        lax.fori_loop(1, GROUP, end, 0)
+        lax.fori_loop(self.low, GROUP, end, 0)
 
 
 def kernel(
-    pat, vals, offs, cov, blk, omat, odat,
+    pat, vals, offs_h, cov, blk_h, omat, odat_h,
     out_dyn, out_off, out_cov, out_fac, out_info,
     cov_v, obs_v, vi, vj, ga, gb, phi, s1, t1, n1, linv_v, s2, linv2_v,
-    g_v, k_v, u_v, o_v, xt, pk, rec, lamt, lamt_a, bz, ba, c_pan, ca, g2a, g2b, g2_v, k2_v,
-    pk2, rec2, fac2, c2, lam2, vec, vec_in, lam, fac, z1, z2, kb_v,
+    g_v, k_v, u_v, o_v, xt, pk, rec, lamt, lamt_a, bz, ba, c_pan, ca, g2a, g2b, g2_v,
+    pk2, rec2, pkl, recl, fac2, c2, vec, vec_in, lam, fac, z1, z2, kb_v, offs, blk, odat,
     obs_s, obs_r, gat_s, gat_r, swap_s, swap_r, z_s, z_r, own,
 ):
     tm, row, obs = lax.axis_index("tm"), lax.axis_index("row"), lax.axis_index("obs")
@@ -299,34 +303,42 @@
     gather_2b = Gather(place, None, g2b, gat_s.at[5], gat_r.at[5], True)
     swap1 = Swap(place, pk, rec, swap_s.at[0], swap_r.at[0], own.at[4])
     swap2 = Swap(place, pk2, rec2, swap_s.at[1], swap_r.at[1], own.at[5])
+    swap3 = Swap(down, pkl, recl, swap_s.at[2], swap_r.at[2], None)
     up_lam = z_copy(0, lamt, lamt_a, up)
     up_b = z_copy(1, bz, ba, up)
-    up_cov = z_copy(2, c_pan, ca, up)
-    down_dyn = z_copy(3, lam2, out_dyn.at[0], down)
-    down_cov = z_copy(4, c2, out_cov.at[0], down)
-    down_fac = z_copy(5, fac2, out_fac.at[0, :, 0 : 2 * BW], down)
-    down_vec = z_copy(6, vec, vec_in, down)
+    def chunk(n):
+        return pl.ds(n * CHUNK, CHUNK)
+
+    up_cov = [z_copy(8 + n, c_pan.at[:, chunk(n)], ca.at[:, chunk(n)], up) for n in range(ST // CHUNK)]
+    down_cov = [
+        z_copy(4 + n, c2.at[:, chunk(n)], out_cov.at[0, :, chunk(n)], down) for n in range(ST // CHUNK)
+    ]
+    down_fac = z_copy(2, fac2, out_fac.at[0, :, 0 : 2 * BW], down)
+    down_vec = z_copy(3, vec, vec_in, down)
 
     local_cov = pltpu.make_async_copy(cov, cov_v, own.at[0])
     local_i = pltpu.make_async_copy(vals.at[0], vi.at[core, x, obs], own.at[1])
     local_j = pltpu.make_async_copy(vals.at[1], vj.at[core, obs, x], own.at[2])
     local_obs = pltpu.make_async_copy(omat, obs_v.at[:, obs], own.at[3])
+    tiny = [
+        pltpu.make_async_copy(a, b, own.at[9 + n])
+        for n, (a, b) in enumerate([(offs_h, offs), (odat_h, odat), (blk_h, blk)])
+    ]
     local_obs.start()
+    for one in tiny:
+        one.start()
     local_cov.start()
     local_i.start()
     local_j.start()
 
     barrier = pltpu.get_barrier_semaphore()
 
-    def greet(off, carry):
-        t = lax.rem(me + off, GROUP)
-        pl.semaphore_signal(barrier, inc=1, device_id=(tm, t // SIDE, lax.rem(t, SIDE)), device_id_type=MESH)
-        return carry
-
-    lax.fori_loop(1, GROUP, greet, 0)
-    pl.semaphore_signal(barrier, inc=1, device_id=up, device_id_type=MESH)
-    pl.semaphore_signal(barrier, inc=1, device_id=down, device_id_type=MESH)
-    pl.semaphore_wait(barrier, GROUP + 1)
+    partners = [(tm, row, lax.rem(obs + d, SIDE)) for d in range(1, SIDE)]
+    partners += [(tm, 2 * lax.rem(x + d, SIDE) + core, obs) for d in range(1, SIDE)]
+    partners += [(tm, 2 * x + 1 - core, obs), up, down]
+    for partner in partners:
+        pl.semaphore_signal(barrier, inc=1, device_id=partner, device_id_type=MESH)
+    pl.semaphore_wait(barrier, len(partners))
 
     for d in range(1, SIDE):
         obs_copy(1, d).start()
@@ -336,6 +348,8 @@
     gather_j.phase1()
 
     local_obs.wait()
+    for one in tiny:
+        one.wait()
     for d in range(1, SIDE):
         obs_copy(1, d).wait_recv()
     for d, part in enumerate(factor_rows(blk[1:2, :], obs_v[1].reshape(BW, 2 * BW))):
@@ -395,7 +409,7 @@
         for d in range(NB):
             part = jnp.zeros((BW, BW), F32) if c == 0 else o_v[d]
             for n in range(3):
-                part = part + is_block(pat[0, c, n], d) * t[:, n * BW : (n + 1) * BW]
+                part = part + is_block(pat[n, 0, c], d) * t[:, n * BW : (n + 1) * BW]
             o_v[d] = part
     for d in range(NB):
         u_v[d] = mm(linv, o_v[d], NN)
@@ -406,7 +420,7 @@
         rows = rows_i(c)
         w = jnp.zeros((BW, BW), F32)
         for n in range(3):
-            w = w + is_block(pat[0, c, n], row) * rows[:, n * BW : (n + 1) * BW]
+            w = w + is_block(pat[n, 0, c], row) * rows[:, n * BW : (n + 1) * BW]
         t1[...] = w.T
         sl = slice(c * BW, (c + 1) * BW)
         xt[c] = jnp.concatenate([p[:, sl], t1[pl.ds(lo, PAN), :] - drop[:, sl], xrow[:, sl]], axis=0)
@@ -434,10 +448,17 @@
     info = mm(solved, upper, NT) + mm(zeta_i, prior, NT)
     swap1.finish()
 
-    unpack(rec, 0, z1)
+    def send_up(n):
+        @pl.when(jnp.logical_not(odd))
+        def _():
+            up_cov[n].start()
+
+    unpack(rec, z1)
     for c in range(NB):
         sl = slice(c * BW, (c + 1) * BW)
         c_pan[:, sl] = dyn_times(z1, pat, rows_j, 1, c).T + cov_v[1, :, sl]
+        if c % 2 == 1:
+            send_up(c // 2)
 
     def my_panel(full):
         put_blocks(o_v.at[:, 0:8, :], full)
@@ -446,19 +467,26 @@
 
     @pl.when(jnp.logical_not(odd))
     def _():
-        up_cov.start()
         pieces = pltpu.make_async_copy(fac.at[:, 0 : 2 * BW], out_fac.at[0, :, 2 * BW :], own.at[6])
         pieces.start()
         pieces.wait()
         down_vec.wait_recv()
         out_off[...] = vec_in[0:1, 0:PAN]
         out_info[...] = info[0:1, :] + vec_in[1:2, 0:PAN]
-        down_dyn.wait_recv()
-        down_cov.wait_recv()
+        swap3.finish()
+        unpack(recl, z1)
+        for c in range(NB):
+            lam[:, c * BW : (c + 1) * BW] = z1[c].reshape(BW, PAN).T
+        dyn_out = pltpu.make_async_copy(lam, out_dyn.at[0], own.at[8])
+        dyn_out.start()
+        dyn_out.wait()
+        for one in down_cov:
+            one.wait_recv()
         down_fac.wait_recv()
         up_lam.wait_send()
         up_b.wait_send()
-        up_cov.wait_send()
+        for one in up_cov:
+            one.wait_send()
 
     @pl.when(odd)
     def _():
@@ -475,12 +503,12 @@
         lam_parts = [jnp.zeros((PAN, BW), F32) for _ in range(NB)]
         ak = jnp.zeros((PAN, BW), F32)
         for n in range(3):
-            b = pat[1, row, n]
+            b = pat[n, 1, row]
             block = vj[core, obs, x, :, n * BW : (n + 1) * BW]
             mine = halves(block)
             t = mm(mine, vi[lax.rem(b, 2), lax.div(b, 2)].reshape(BW, 3 * BW), NN)
             for m in range(3):
-                at = pat[0, b, m]
+                at = pat[m, 0, b]
                 for d in range(NB):
                     lam_parts[d] = lam_parts[d] + is_block(at, d) * t[:, m * BW : (m + 1) * BW]
             ak = ak + mm(mine, kb_v[b], NN)
@@ -490,14 +518,22 @@
         dyn_out = pltpu.make_async_copy(lam, out_dyn.at[0], own.at[8])
         dyn_out.start()
 
-        up_cov.wait_recv()
         u = jnp.concatenate([u_v[d] for d in range(NB)], axis=1)
         phi_b = halves(jnp.concatenate([u, phi[0]], axis=0))
-        gain2 = mm(ca[...], phi_b, NT)
+        gain2 = jnp.zeros((PAN, 2 * BW), F32)
+        for n in range(ST // CHUNK):
+            up_cov[n].wait_recv()
+            part = tuple(h[:, n * CHUNK : (n + 1) * CHUNK] for h in phi_b)
+            gain2 = gain2 + mm(ca[:, chunk(n)], part, NT)
         g2a[core, x, obs] = gain2[:, :BW]
         g2b[core, obs, x] = gain2[:, BW:]
         gather_2a.phase1()
         gather_2b.phase1()
+        la, bp = lamt_a[...], ba[...]
+        start = jnp.concatenate([ca[...], la, bp], axis=0)
+        across = mm(start[PAN:], phi_b, NT)
+        seen = across[:PAN]
+        resid = jnp.concatenate([solved, zeta_i], axis=1) - across[PAN:]
         gather_2a.phase2()
         gather_2b.phase2()
         gather_2a.phase3()
@@ -511,38 +547,28 @@
         s2[...] = eye(2 * BW) + mm(phi_b, g2, NN)
         chol_inverse_2(s2, linv2_v, t1, n1)
         linv2 = halves(linv2_v[...])
-        k2 = mm(g2, linv2, NT)
-        k2_v[...] = k2
-        k2h = halves(k2)
-        p2 = ca[...] - mm(k2_v[pl.ds(row0, PAN), :], k2h, NT)
-        la = lamt_a[...]
-        upper2 = mm(mm(la, phi_b, NT), linv2, NT)
-        fac2[...] = upper2
+        ahead = mm(jnp.concatenate([g2_v[pl.ds(row0, PAN), :], seen, resid], axis=0), linv2, NT)
+        fac2[...] = ahead[PAN : 2 * PAN]
         down_fac.start()
-        mt = la - mm(upper2, k2h, NT)
-        zeta = jnp.concatenate([solved, zeta_i], axis=1)
-        bp = ba[...]
-        solved2 = mm(zeta - mm(bp, phi_b, NT), linv2, NT)
-        xs = jnp.concatenate([p2, mt, bp + mm(solved2, k2h, NT)], axis=0)
+        solved2 = ahead[2 * PAN :]
+        sign = jnp.where(lax.broadcasted_iota(jnp.int32, (2 * PAN + 8, 1), 0) < 2 * PAN, -1.0, 1.0)
+        xs = start + mm(sign * mm(ahead, linv2, NN), g2, NT)
         put_blocks(xt, xs)
         h = jnp.concatenate(times_dyn_t(xt, pat, rows_i, 0), axis=1)
         put_blocks(xt, h - mm(mm(xs, u, NT), k_v[...], NT))
         y2 = jnp.concatenate(times_dyn_t(xt, pat, rows_j, 1), axis=1)
         for q, part in enumerate(pack(y2[:PAN, :])):
-            pk2[q, 0:8] = part
+            pk2[q] = part
+        swap2.start()
         for q, part in enumerate(pack(y2[PAN : 2 * PAN, :])):
-            pk2[q, 8:16] = part
-        swap2.start()
+            pkl[q] = part
+        swap3.start()
         vec[...] = jnp.zeros((8, BW), F32)
         vec[0:1, 0:PAN] = my_panel(y2[2 * PAN :, :] + b_own)
-        vec[1:2, 0:PAN] = mm(solved2, upper2, NT)[0:1, :]
+        vec[1:2, 0:PAN] = mm(solved2, fac2[...], NT)[0:1, :]
         down_vec.start()
         swap2.finish()
-        unpack(rec2, 8, z1)
-        for c in range(NB):
-            lam2[:, c * BW : (c + 1) * BW] = z1[c].reshape(BW, PAN).T
-        down_dyn.start()
-        unpack(rec2, 0, z1)
+        unpack(rec2, z1)
         uz = jnp.zeros((BW, PAN), F32)
         for d in range(NB):
             uz = uz + mm(u_v[d], z1[d].reshape(BW, PAN), NN)
@@ -553,14 +579,16 @@
         for c in range(NB):
             sl = slice(c * BW, (c + 1) * BW)
             c2[:, sl] = dyn_times(z2, pat, rows_j, 1, c).T + c_pan[:, sl]
-        down_cov.start()
+            if c % 2 == 1:
+                down_cov[c // 2].start()
         for one in ones:
             one.wait()
         dyn_out.wait()
         gather_2a.drain()
         gather_2b.drain()
         swap2.drain()
-        for one in (down_fac, down_vec, down_dyn, down_cov):
+        swap3.drain()
+        for one in [down_fac, down_vec] + down_cov:
             one.wait_send()
 
     for e in range(2):
@@ -590,27 +618,45 @@
     vmem(GROUP, 8, BW), vmem(GROUP, 8, BW),
     vmem(PAN, ST), vmem(PAN, ST), vmem(8, ST), vmem(8, ST), vmem(PAN, ST), vmem(PAN, ST),
     vmem(2, SIDE, SIDE, PAN, BW), vmem(2, SIDE, SIDE, PAN, BW),
-    vmem(ST, 2 * BW), vmem(ST, 2 * BW),
-    vmem(GROUP, 16, BW), vmem(GROUP, 16, BW),
-    vmem(PAN, 2 * BW), vmem(PAN, ST), vmem(PAN, ST), vmem(8, BW), vmem(8, BW),
+    vmem(ST, 2 * BW),
+    vmem(GROUP, 8, BW), vmem(GROUP, 8, BW), vmem(GROUP, 8, BW), vmem(GROUP, 8, BW),
+    vmem(PAN, 2 * BW), vmem(PAN, ST), vmem(8, BW), vmem(8, BW),
     vmem(PAN, ST), vmem(PAN, 4 * BW),
     vmem(NB, 4, PAN, PAN), vmem(NB, 4, PAN, PAN), vmem(NB, BW, BW),
-    dma(2, 3), dma(2, 3), dma(6, 10), dma(6, 10), dma(2, GROUP), dma(2, GROUP), dma(7), dma(7), dma(9),
+    vmem(2, PAN), pltpu.VMEM((2, BW), jnp.int32), vmem(2, PAN),
+    dma(2, 3), dma(2, 3), dma(6, 10), dma(6, 10), dma(3, GROUP), dma(3, GROUP), dma(12), dma(12), dma(12),
 ]
 
 
-def per_device(*args):
+def place_body(*refs):
+    n = len(refs) // 2
+    sems = refs[-1]
+    copies = [pltpu.make_async_copy(refs[i], refs[n + i], sems.at[i]) for i in range(n)]
+    for one in copies:
+        one.start()
+    for one in copies:
+        one.wait()
+
+
+def per_device(dyn_pattern, *rest):
     outs = [(1, PAN, ST), (1, PAN), (1, PAN, ST), (1, PAN, 4 * BW), (1, PAN)]
-    return pl.pallas_call(
+    found = pl.pallas_call(
         kernel,
         out_shape=[jax.ShapeDtypeStruct(s, F32) for s in outs],
-        in_specs=[SM, ANY, VM, ANY, VM, ANY, VM],
+        in_specs=[SM] + [ANY] * 6,
         out_specs=[ANY, VM, ANY, ANY, VM],
         scratch_shapes=SCRATCH,
         compiler_params=pltpu.CompilerParams(
-            collective_id=0, has_side_effects=True, vmem_limit_bytes=50 << 20
+            collective_id=0, has_side_effects=True, vmem_limit_bytes=60 << 20
         ),
-    )(*args)
+    )(jnp.transpose(dyn_pattern, (2, 0, 1)), *rest)
+    return pl.pallas_call(
+        place_body,
+        out_shape=[jax.ShapeDtypeStruct(s, F32) for s in outs],
+        in_specs=[VM] * len(outs),
+        out_specs=[ANY] * len(outs),
+        scratch_shapes=[dma(len(outs))],
+    )(*found)
 
 
 def solution(mesh):

time: 100 us -> 90 us (0.900)
  local copies, waits for them, and re-layouts: 6.43 us -> 0 us
  Pallas kernels: 92.6 us -> 89.1 us
    unnamed x18 -> x0, local copies, waits for them, and re-layouts: 6.43 us -> none
    pallas_call x1, Pallas kernels: 92.6 us -> 87.3 us  [per_device(): pl.pallas_call(kernel, out_shape=[jax.ShapeDtypeStruct(s, F32) for s in o...]
    pallas_call x0 -> x1, Pallas kernels: none -> 1.78 us  [per_device(): pl.pallas_call(place_body, out_shape=[jax.ShapeDtypeStruct(s, F32) for s...]
where the time goes in v2:
time: 90 us; the launch traced here: 89.9 us
  Pallas kernels  89.1 us (99%)
    pallas_call x1, Pallas kernels, per_device(): pl.pallas_call(kernel, out_shape=[jax.ShapeDtypeStruct(s, F32) for s in o...  87.3 us

profile of v2, /device:TPU:1, one launch (start us, length us, event | category | flops | bytes accessed | tf_op | source)
XLA Modules:
  0.0 89.9 jit_solution(13717068904911364880)
XLA Ops:
  0.6 87.3 %shard_map.110 = (f32[1,32,1024]{2,1,0:T(8,128)}, f32[1,32]{1,0:T(1,128)}, f32[1,32,1024]{2,1,0:T(8,128)}, f32[1,32,512]{2,1,0:T(8,128)}, f32[1,32]{1,0:T(1,128)}) custom-call(s32[3,2,8]{2,1,0:T(2,128)} %bitcast.1, f32[2,32,384]{2,1,0:T(8,128)} %vals.1, f32[2,32]{1,0:T(2,128)} %offs_h.1, f32[2,32,1024]{2,1,0:T(8,128)} %cov.1, s32[2,128]{1,0:T(2,128)} %blk_h.1, ...), custom_call_target="tpu_custom_call" | custom-call | tf_op jit(solution)/shard_map/pallas_call | solution.py:643
  88.0 1.8 %shard_map.111 = (f32[1,32,1024]{2,1,0:T(8,128)}, f32[1,32]{1,0:T(1,128)}, f32[1,32,1024]{2,1,0:T(8,128)}, f32[1,32,512]{2,1,0:T(8,128)}, f32[1,32]{1,0:T(1,128)}) custom-call(f32[1,32,1024]{2,1,0:T(8,128)} %get-tuple-element.10.refs_0_, f32[1,32]{1,0:T(1,128)} %get-tuple-element.11.refs_1_, f32[1,32,1024]{2,1,0:T(8,128)} %get-tuple-element.12.refs_2_, ...), custom_call_target="tpu_custom_call" | custom-call | tf_op jit(solution)/shard_map/pallas_call | solution.py:653

commit v3 on v2

--- a/solution.py
+++ b/solution.py
@@ -155,12 +155,13 @@
 
 
 class Gather:
-    def __init__(self, place, src, buf, send, recv, swapped):
+    def __init__(self, place, src, buf, send, recv, swapped, ring=False):
         tm, row, obs = place
         x, core = row // 2, lax.rem(row, 2)
         self.core, self.buf, self.src = core, buf, src
         self.i, self.j = (obs, x) if swapped else (x, obs)
-        self.send, self.recv = send, recv
+        self.send, self.recv, self.ring = send, recv, ring
+        self.direct = (1, 3) if ring else (1, 2, 3)
 
         def device(i, j, c):
             xx, yy = (j, i) if swapped else (i, j)
@@ -195,12 +196,29 @@
     def phase2(self):
         for d in range(1, SIDE):
             self.first(d).wait_recv()
-        for d in range(1, SIDE):
+        for d in self.direct:
             self.second(d).start()
         self.across(0).start()
 
+    def onward(self, d):
+        half = pl.ds(0, SIDE // 2) if d == 1 else pl.ds(SIDE // 2, SIDE // 2)
+        part = self.buf.at[self.core, lax.rem(self.i + SIDE - d, SIDE), half]
+        return self.copy(part, part, 4 if d == 1 else 10, self.device(lax.rem(self.i + d, SIDE), self.j, self.core))
+
+    def pass_on(self):
+        for d in (1, 3):
+            self.second(d).wait_recv()
+            self.onward(d).start()
+        for d in (1, 3):
+            self.across(d).start()
+
     def phase3(self):
-        for d in range(1, SIDE):
+        if self.ring:
+            for d in (1, 3):
+                self.onward(d).wait_recv()
+            self.across(2).start()
+            return
+        for d in self.direct:
             self.second(d).wait_recv()
             self.across(d).start()
 
@@ -211,62 +229,62 @@
     def drain(self):
         for d in range(1, SIDE):
             self.first(d).wait_send()
+        for d in self.direct:
             self.second(d).wait_send()
+        if self.ring:
+            for d in (1, 3):
+                self.onward(d).wait_send()
         for d in range(SIDE):
             self.across(d).wait_send()
 
 
 class Swap:
-    def __init__(self, place, src, dst, send, recv, own):
+    def __init__(self, place, src, dst, sem, n, own):
         self.tm, row, obs = place
         self.me = row * SIDE + obs
-        self.src, self.dst, self.send, self.recv, self.own = src, dst, send, recv, own
-        self.low = 0 if own is None else 1
-
-    def copy(self, off):
-        t = lax.rem(self.me + off, GROUP)
-        return pltpu.make_async_remote_copy(
-            src_ref=self.src.at[t], dst_ref=self.dst.at[self.me],
-            send_sem=self.send.at[off], recv_sem=self.recv.at[off],
-            device_id=(self.tm, t // SIDE, lax.rem(t, SIDE)), device_id_type=MESH,
-        )
+        self.src, self.dst, self.own = src, dst, own
+        self.send, self.recv = sem.at[2 * n], sem.at[2 * n + 1]
+        self.rows = [lax.rem(row + d, NB) for d in range(NB)]
+        self.cols = [lax.rem(obs + d, SIDE) for d in range(SIDE)]
+
+    def start(self):
+        for dr in range(NB):
+            for do in range(SIDE):
+                if dr + do > 0:
+                    r, o = self.rows[dr], self.cols[do]
+                    pltpu.make_async_remote_copy(
+                        src_ref=self.src.at[r * SIDE + o], dst_ref=self.dst.at[self.me],
+                        send_sem=self.send, recv_sem=self.recv,
+                        device_id=(self.tm, r, o), device_id_type=MESH,
+                    ).start()
+        self.mine().start()
 
     def mine(self):
         return pltpu.make_async_copy(self.src.at[self.me], self.dst.at[self.me], self.own)
 
-    def start(self):
-        def begin(off, carry):
-            self.copy(off).start()
-            return carry
-
-        lax.fori_loop(self.low, GROUP, begin, 0)
-        if self.low:
-            self.mine().start()
+    def total(self):
+        blocks = pl.ds(0, GROUP - 1)
+        return pltpu.make_async_remote_copy(
+            src_ref=self.src.at[blocks], dst_ref=self.dst.at[blocks],
+            send_sem=self.send, recv_sem=self.recv,
+            device_id=(self.tm, self.rows[1], self.cols[0]), device_id_type=MESH,
+        )
 
     def finish(self):
-        def end(off, carry):
-            self.copy(off).wait_recv()
-            return carry
-
-        if self.low:
-            self.mine().wait()
-        lax.fori_loop(self.low, GROUP, end, 0)
+        self.mine().wait()
+        self.total().wait_recv()
 
     def drain(self):
-        def end(off, carry):
-            self.copy(off).wait_send()
-            return carry
-
-        lax.fori_loop(self.low, GROUP, end, 0)
+        self.total().wait_send()
 
 
 def kernel(
     pat, vals, offs_h, cov, blk_h, omat, odat_h,
     out_dyn, out_off, out_cov, out_fac, out_info,
-    cov_v, obs_v, vi, vj, ga, gb, phi, s1, t1, n1, linv_v, s2, linv2_v,
+    cov_v, obs_v, vi, vj, ga, gb, gs, phi, s1, t1, n1, linv_v, s2, linv2_v,
     g_v, k_v, u_v, o_v, xt, pk, rec, lamt, lamt_a, bz, ba, c_pan, ca, g2a, g2b, g2_v,
-    pk2, rec2, pkl, recl, fac2, c2, vec, vec_in, lam, fac, z1, z2, kb_v, offs, blk, odat,
-    obs_s, obs_r, gat_s, gat_r, swap_s, swap_r, z_s, z_r, own,
+    pk2, rec2, pkl, recl, lamt2, lamt2_in, fac2, c2, vec, vec_in, lam, fac, z1, z2, kb_v, offs, blk, odat,
+    obs_s, obs_r, gat_s, gat_r, swap, z_s, z_r, own,
 ):
     tm, row, obs = lax.axis_index("tm"), lax.axis_index("row"), lax.axis_index("obs")
     place = (tm, row, obs)
@@ -295,15 +313,16 @@
             src_ref=src, dst_ref=dst, send_sem=z_s.at[n], recv_sem=z_r.at[n], device_id=device, device_id_type=MESH
         )
 
-    gather_i = Gather(place, vals.at[0], vi, gat_s.at[0], gat_r.at[0], False)
-    gather_j = Gather(place, vals.at[1], vj, gat_s.at[1], gat_r.at[1], True)
+    gather_i = Gather(place, vals.at[0], vi, gat_s.at[0], gat_r.at[0], False, True)
+    gather_j = Gather(place, vals.at[1], vj, gat_s.at[1], gat_r.at[1], True, True)
     gather_ga = Gather(place, None, ga, gat_s.at[2], gat_r.at[2], False)
     gather_gb = Gather(place, None, gb, gat_s.at[3], gat_r.at[3], True)
+    gather_gs = Gather(place, None, gs, gat_s.at[6], gat_r.at[6], False)
     gather_2a = Gather(place, None, g2a, gat_s.at[4], gat_r.at[4], False)
     gather_2b = Gather(place, None, g2b, gat_s.at[5], gat_r.at[5], True)
-    swap1 = Swap(place, pk, rec, swap_s.at[0], swap_r.at[0], own.at[4])
-    swap2 = Swap(place, pk2, rec2, swap_s.at[1], swap_r.at[1], own.at[5])
-    swap3 = Swap(down, pkl, recl, swap_s.at[2], swap_r.at[2], None)
+    swap1 = Swap(place, pk, rec, swap, 0, own.at[4])
+    swap2 = Swap(place, pk2, rec2, swap, 1, own.at[5])
+    swap3 = Swap(place, pkl, recl, swap, 2, own.at[5])
     up_lam = z_copy(0, lamt, lamt_a, up)
     up_b = z_copy(1, bz, ba, up)
     def chunk(n):
@@ -315,6 +334,7 @@
     ]
     down_fac = z_copy(2, fac2, out_fac.at[0, :, 0 : 2 * BW], down)
     down_vec = z_copy(3, vec, vec_in, down)
+    down_lam = z_copy(12, lamt2, lamt2_in, down)
 
     local_cov = pltpu.make_async_copy(cov, cov_v, own.at[0])
     local_i = pltpu.make_async_copy(vals.at[0], vi.at[core, x, obs], own.at[1])
@@ -342,8 +362,6 @@
 
     for d in range(1, SIDE):
         obs_copy(1, d).start()
-    for d in range(1, SIDE):
-        obs_copy(0, d).start()
     gather_i.phase1()
     gather_j.phase1()
 
@@ -358,17 +376,21 @@
     gain = mm(cov_v[0], phi[1], NT)
     ga[core, x, obs] = gain[0:16]
     small = jnp.concatenate([offs[...], odat[...]], axis=0)
-    gb[core, obs, x, 0:16] = gain[16:32]
-    gb[core, obs, x, 16:24] = jnp.zeros((8, BW), F32)
-    gb[core, obs, x, 16:20, 0:PAN] = small
+    gb[core, obs, x] = gain[16:32]
+    gs[core, x, obs] = jnp.zeros((8, BW), F32)
+    gs[core, x, obs, 0:4, 0:PAN] = small
     gather_ga.phase1()
     gather_gb.phase1()
+    for d in range(1, SIDE):
+        obs_copy(0, d).start()
+    gather_gs.phase1()
     gather_ga.phase2()
     gather_gb.phase2()
     local_i.wait()
     local_j.wait()
     gather_i.phase2()
     gather_j.phase2()
+    gather_gs.phase2()
     gather_ga.phase3()
     gather_gb.phase3()
     for d in range(1, SIDE):
@@ -377,16 +399,12 @@
         phi[0, :, d * BW : (d + 1) * BW] = part
     gather_ga.finish()
     gather_gb.finish()
-
-    vecs = []
+    gather_i.pass_on()
+    gather_j.pass_on()
+
     for c in range(NB):
-        both = jnp.concatenate([ga[c % 2, c // 2], gb[c % 2, :, c // 2, 0:16]], axis=1)
+        both = jnp.concatenate([ga[c % 2, c // 2], gb[c % 2, :, c // 2]], axis=1)
         g_v[c * BW : (c + 1) * BW, :] = both.reshape(BW, BW)
-        vecs.append(jnp.concatenate([gb[c % 2, o, c // 2, 16:24, 0:PAN] for o in range(SIDE)], axis=1))
-    zeta_i = jnp.broadcast_to(vecs[0][2:3, :], (8, BW))
-    zeta_j = jnp.broadcast_to(vecs[0][3:4, :], (8, BW))
-    b_i = jnp.concatenate([jnp.broadcast_to(v[0:1, :], (8, BW)) for v in vecs], axis=1)
-    b_j = jnp.concatenate([jnp.broadcast_to(v[1:2, :], (8, BW)) for v in vecs], axis=1)
     g = halves(g_v[...])
     phi_j = halves(phi[1])
     s1[...] = eye(BW) + mm(phi_j, g, NN)
@@ -398,10 +416,19 @@
         kb_v[c] = k[c * BW : (c + 1) * BW, :]
     kh = halves(k)
     p = cov_v[0] - mm(k_v[pl.ds(row0, PAN), :], kh, NT)
+    gather_i.phase3()
+    gather_j.phase3()
+    gather_gs.phase3()
+    gather_gs.finish()
+    vecs = [
+        jnp.concatenate([gs[c % 2, c // 2, o, :, 0:PAN] for o in range(SIDE)], axis=1) for c in range(NB)
+    ]
+    zeta_i = jnp.broadcast_to(vecs[0][2:3, :], (8, BW))
+    zeta_j = jnp.broadcast_to(vecs[0][3:4, :], (8, BW))
+    b_i = jnp.concatenate([jnp.broadcast_to(v[0:1, :], (8, BW)) for v in vecs], axis=1)
+    b_j = jnp.concatenate([jnp.broadcast_to(v[1:2, :], (8, BW)) for v in vecs], axis=1)
     solved = mm(zeta_j - mm(b_i, phi_j, NT), linv, NT)
     xrow = b_i + mm(solved, kh, NT)
-    gather_i.phase3()
-    gather_j.phase3()
     gather_i.finish()
 
     for c in range(NB):
@@ -470,6 +497,10 @@
         pieces = pltpu.make_async_copy(fac.at[:, 0 : 2 * BW], out_fac.at[0, :, 2 * BW :], own.at[6])
         pieces.start()
         pieces.wait()
+        down_lam.wait_recv()
+        for q, part in enumerate(pack(lamt2_in[...])):
+            pkl[q] = part
+        swap3.start()
         down_vec.wait_recv()
         out_off[...] = vec_in[0:1, 0:PAN]
         out_info[...] = info[0:1, :] + vec_in[1:2, 0:PAN]
@@ -480,6 +511,7 @@
         dyn_out = pltpu.make_async_copy(lam, out_dyn.at[0], own.at[8])
         dyn_out.start()
         dyn_out.wait()
+        swap3.drain()
         for one in down_cov:
             one.wait_recv()
         down_fac.wait_recv()
@@ -560,9 +592,8 @@
         for q, part in enumerate(pack(y2[:PAN, :])):
             pk2[q] = part
         swap2.start()
-        for q, part in enumerate(pack(y2[PAN : 2 * PAN, :])):
-            pkl[q] = part
-        swap3.start()
+        lamt2[...] = y2[PAN : 2 * PAN, :]
+        down_lam.start()
         vec[...] = jnp.zeros((8, BW), F32)
         vec[0:1, 0:PAN] = my_panel(y2[2 * PAN :, :] + b_own)
         vec[1:2, 0:PAN] = mm(solved2, fac2[...], NT)[0:1, :]
@@ -587,14 +618,13 @@
         gather_2a.drain()
         gather_2b.drain()
         swap2.drain()
-        swap3.drain()
-        for one in [down_fac, down_vec] + down_cov:
+        for one in [down_fac, down_vec, down_lam] + down_cov:
             one.wait_send()
 
     for e in range(2):
         for d in range(1, SIDE):
             obs_copy(e, d).wait_send()
-    for one in (gather_i, gather_j, gather_ga, gather_gb):
+    for one in (gather_i, gather_j, gather_ga, gather_gb, gather_gs):
         one.drain()
     swap1.drain()
 
@@ -610,7 +640,7 @@
 SCRATCH = [
     vmem(2, PAN, ST), vmem(2, SIDE, PAN, 2 * BW),
     vmem(2, SIDE, SIDE, PAN, 3 * BW), vmem(2, SIDE, SIDE, PAN, 3 * BW),
-    vmem(2, SIDE, SIDE, 16, BW), vmem(2, SIDE, SIDE, 24, BW),
+    vmem(2, SIDE, SIDE, 16, BW), vmem(2, SIDE, SIDE, 16, BW), vmem(2, SIDE, SIDE, 8, BW),
     vmem(2, BW, ST),
     vmem(BW, BW), vmem(BW, BW), vmem(BW, BW), vmem(BW, BW),
     vmem(2 * BW, 2 * BW), vmem(2 * BW, 2 * BW),
@@ -620,11 +650,12 @@
     vmem(2, SIDE, SIDE, PAN, BW), vmem(2, SIDE, SIDE, PAN, BW),
     vmem(ST, 2 * BW),
     vmem(GROUP, 8, BW), vmem(GROUP, 8, BW), vmem(GROUP, 8, BW), vmem(GROUP, 8, BW),
+    vmem(PAN, ST), vmem(PAN, ST),
     vmem(PAN, 2 * BW), vmem(PAN, ST), vmem(8, BW), vmem(8, BW),
     vmem(PAN, ST), vmem(PAN, 4 * BW),
     vmem(NB, 4, PAN, PAN), vmem(NB, 4, PAN, PAN), vmem(NB, BW, BW),
     vmem(2, PAN), pltpu.VMEM((2, BW), jnp.int32), vmem(2, PAN),
-    dma(2, 3), dma(2, 3), dma(6, 10), dma(6, 10), dma(3, GROUP), dma(3, GROUP), dma(12), dma(12), dma(12),
+    dma(2, 3), dma(2, 3), dma(7, 12), dma(7, 12), dma(6), dma(13), dma(13), dma(12),
 ]
 
 

time: 90 us -> 88.5 us (0.983)
  Pallas kernels: 89.1 us -> 87.6 us
    pallas_call x1, Pallas kernels: 87.3 us -> 85.8 us  [per_device(): pl.pallas_call(kernel, out_shape=[jax.ShapeDtypeStruct(s, F32) for s in o...]
where the time goes in v3:
time: 88.5 us; the launch traced here: 88.4 us
  Pallas kernels  87.6 us (99%)
    pallas_call x1, Pallas kernels, per_device(): pl.pallas_call(kernel, out_shape=[jax.ShapeDtypeStruct(s, F32) for s in o...  85.8 us
    pallas_call x1, Pallas kernels, per_device(): pl.pallas_call(place_body, out_shape=[jax.ShapeDtypeStruct(s, F32) for s...  1.78 us

profile of v3, /device:TPU:1, one launch (start us, length us, event | category | flops | bytes accessed | tf_op | source)
XLA Modules:
  0.0 88.4 jit_solution(9300059933207966388)
XLA Ops:
  0.6 85.8 %shard_map.110 = (f32[1,32,1024]{2,1,0:T(8,128)}, f32[1,32]{1,0:T(1,128)}, f32[1,32,1024]{2,1,0:T(8,128)}, f32[1,32,512]{2,1,0:T(8,128)}, f32[1,32]{1,0:T(1,128)}) custom-call(s32[3,2,8]{2,1,0:T(2,128)} %bitcast.1, f32[2,32,384]{2,1,0:T(8,128)} %vals.1, f32[2,32]{1,0:T(2,128)} %offs_h.1, f32[2,32,1024]{2,1,0:T(8,128)} %cov.1, s32[2,128]{1,0:T(2,128)} %blk_h.1, ...), custom_call_target="tpu_custom_call" | custom-call | tf_op jit(solution)/shard_map/pallas_call | solution.py:674
  86.4 1.8 %shard_map.111 = (f32[1,32,1024]{2,1,0:T(8,128)}, f32[1,32]{1,0:T(1,128)}, f32[1,32,1024]{2,1,0:T(8,128)}, f32[1,32,512]{2,1,0:T(8,128)}, f32[1,32]{1,0:T(1,128)}) custom-call(f32[1,32,1024]{2,1,0:T(8,128)} %get-tuple-element.10.refs_0_, f32[1,32]{1,0:T(1,128)} %get-tuple-element.11.refs_1_, f32[1,32,1024]{2,1,0:T(8,128)} %get-tuple-element.12.refs_2_, ...), custom_call_target="tpu_custom_call" | custom-call | tf_op jit(solution)/shard_map/pallas_call | solution.py:684

commit v4 on v3

--- a/solution.py
+++ b/solution.py
@@ -40,12 +40,14 @@
     return jnp.where(rows == cols, 1.0, 0.0).astype(F32)
 
 
-def chol_inverse(s_ref, n_ref):
+def chol_inverse(s_ref, n_ref, ahead_of_last=None):
     n_ref[...] = eye(BW)
     sub = lax.broadcasted_iota(jnp.int32, (8, BW), 0)
     lane = lax.broadcasted_iota(jnp.int32, (32, BW), 1)
 
     def panel(b, carry):
+        if ahead_of_last is not None:
+            pl.when(b == 3)(ahead_of_last)
         k0 = pl.multiple_of(b * 32, 32)
         r = [s_ref[pl.ds(k0 + 8 * t, 8), :] for t in range(4)]
         n = [n_ref[pl.ds(k0 + 8 * t, 8), :] for t in range(4)]
@@ -381,22 +383,18 @@
     gs[core, x, obs, 0:4, 0:PAN] = small
     gather_ga.phase1()
     gather_gb.phase1()
-    for d in range(1, SIDE):
-        obs_copy(0, d).start()
-    gather_gs.phase1()
     gather_ga.phase2()
     gather_gb.phase2()
+    gather_gs.phase1()
     local_i.wait()
     local_j.wait()
     gather_i.phase2()
     gather_j.phase2()
-    gather_gs.phase2()
     gather_ga.phase3()
     gather_gb.phase3()
     for d in range(1, SIDE):
-        obs_copy(0, d).wait_recv()
-    for d, part in enumerate(factor_rows(blk[0:1, :], obs_v[0].reshape(BW, 2 * BW))):
-        phi[0, :, d * BW : (d + 1) * BW] = part
+        obs_copy(0, d).start()
+    gather_gs.phase2()
     gather_ga.finish()
     gather_gb.finish()
     gather_i.pass_on()
@@ -408,7 +406,12 @@
     g = halves(g_v[...])
     phi_j = halves(phi[1])
     s1[...] = eye(BW) + mm(phi_j, g, NN)
-    chol_inverse(s1, linv_v)
+
+    def hand_over():
+        for one in (gather_i, gather_j, gather_gs):
+            one.phase3()
+
+    chol_inverse(s1, linv_v, hand_over)
     linv = halves(linv_v[...])
     k = mm(g, linv, NT)
     k_v[...] = k
@@ -416,9 +419,6 @@
         kb_v[c] = k[c * BW : (c + 1) * BW, :]
     kh = halves(k)
     p = cov_v[0] - mm(k_v[pl.ds(row0, PAN), :], kh, NT)
-    gather_i.phase3()
-    gather_j.phase3()
-    gather_gs.phase3()
     gather_gs.finish()
     vecs = [
         jnp.concatenate([gs[c % 2, c // 2, o, :, 0:PAN] for o in range(SIDE)], axis=1) for c in range(NB)
@@ -465,6 +465,10 @@
         up_lam.start()
         up_b.start()
 
+    for d in range(1, SIDE):
+        obs_copy(0, d).wait_recv()
+    for d, part in enumerate(factor_rows(blk[0:1, :], obs_v[0].reshape(BW, 2 * BW))):
+        phi[0, :, d * BW : (d + 1) * BW] = part
     for d in range(NB):
         o_v[d] = phi[0, :, d * BW : (d + 1) * BW]
     t1[...] = o_v[row].T

time: 88.5 us -> 87.7 us (level)
  no operation moved by 1% of the time
where the time goes in v4:
time: 87.7 us; the launch traced here: 87.6 us
  Pallas kernels  86.8 us (99%)
    pallas_call x1, Pallas kernels, per_device(): pl.pallas_call(kernel, out_shape=[jax.ShapeDtypeStruct(s, F32) for s in o...  85 us
    pallas_call x1, Pallas kernels, per_device(): pl.pallas_call(place_body, out_shape=[jax.ShapeDtypeStruct(s, F32) for s...  1.78 us

profile of v4, /device:TPU:1, one launch (start us, length us, event | category | flops | bytes accessed | tf_op | source)
XLA Modules:
  0.0 87.6 jit_solution(16300209128051820244)
XLA Ops:
  0.6 85.0 %shard_map.110 = (f32[1,32,1024]{2,1,0:T(8,128)}, f32[1,32]{1,0:T(1,128)}, f32[1,32,1024]{2,1,0:T(8,128)}, f32[1,32,512]{2,1,0:T(8,128)}, f32[1,32]{1,0:T(1,128)}) custom-call(s32[3,2,8]{2,1,0:T(2,128)} %bitcast.1, f32[2,32,384]{2,1,0:T(8,128)} %vals.1, f32[2,32]{1,0:T(2,128)} %offs_h.1, f32[2,32,1024]{2,1,0:T(8,128)} %cov.1, s32[2,128]{1,0:T(2,128)} %blk_h.1, ...), custom_call_target="tpu_custom_call" | custom-call | tf_op jit(solution)/shard_map/pallas_call | solution.py:678
  85.7 1.8 %shard_map.111 = (f32[1,32,1024]{2,1,0:T(8,128)}, f32[1,32]{1,0:T(1,128)}, f32[1,32,1024]{2,1,0:T(8,128)}, f32[1,32,512]{2,1,0:T(8,128)}, f32[1,32]{1,0:T(1,128)}) custom-call(f32[1,32,1024]{2,1,0:T(8,128)} %get-tuple-element.10.refs_0_, f32[1,32]{1,0:T(1,128)} %get-tuple-element.11.refs_1_, f32[1,32,1024]{2,1,0:T(8,128)} %get-tuple-element.12.refs_2_, ...), custom_call_target="tpu_custom_call" | custom-call | tf_op jit(solution)/shard_map/pallas_call | solution.py:688

commit v5 on v4

--- a/solution.py
+++ b/solution.py
@@ -593,11 +593,11 @@
         h = jnp.concatenate(times_dyn_t(xt, pat, rows_i, 0), axis=1)
         put_blocks(xt, h - mm(mm(xs, u, NT), k_v[...], NT))
         y2 = jnp.concatenate(times_dyn_t(xt, pat, rows_j, 1), axis=1)
+        lamt2[...] = y2[PAN : 2 * PAN, :]
+        down_lam.start()
         for q, part in enumerate(pack(y2[:PAN, :])):
             pk2[q] = part
         swap2.start()
-        lamt2[...] = y2[PAN : 2 * PAN, :]
-        down_lam.start()
         vec[...] = jnp.zeros((8, BW), F32)
         vec[0:1, 0:PAN] = my_panel(y2[2 * PAN :, :] + b_own)
         vec[1:2, 0:PAN] = mm(solved2, fac2[...], NT)[0:1, :]

time: 87.7 us -> 87.7 us (level)
  no operation moved by 1% of the time
where the time goes in v5:
time: 87.7 us; the launch traced here: 87.6 us
  Pallas kernels  86.8 us (99%)
    pallas_call x1, Pallas kernels, per_device(): pl.pallas_call(kernel, out_shape=[jax.ShapeDtypeStruct(s, F32) for s in o...  85 us
    pallas_call x1, Pallas kernels, per_device(): pl.pallas_call(place_body, out_shape=[jax.ShapeDtypeStruct(s, F32) for s...  1.78 us

profile of v5, /device:TPU:1, one launch (start us, length us, event | category | flops | bytes accessed | tf_op | source)
XLA Modules:
  0.0 87.6 jit_solution(7175430894139216819)
XLA Ops:
  0.6 85.0 %shard_map.110 = (f32[1,32,1024]{2,1,0:T(8,128)}, f32[1,32]{1,0:T(1,128)}, f32[1,32,1024]{2,1,0:T(8,128)}, f32[1,32,512]{2,1,0:T(8,128)}, f32[1,32]{1,0:T(1,128)}) custom-call(s32[3,2,8]{2,1,0:T(2,128)} %bitcast.1, f32[2,32,384]{2,1,0:T(8,128)} %vals.1, f32[2,32]{1,0:T(2,128)} %offs_h.1, f32[2,32,1024]{2,1,0:T(8,128)} %cov.1, s32[2,128]{1,0:T(2,128)} %blk_h.1, ...), custom_call_target="tpu_custom_call" | custom-call | tf_op jit(solution)/shard_map/pallas_call | solution.py:678
  85.7 1.8 %shard_map.111 = (f32[1,32,1024]{2,1,0:T(8,128)}, f32[1,32]{1,0:T(1,128)}, f32[1,32,1024]{2,1,0:T(8,128)}, f32[1,32,512]{2,1,0:T(8,128)}, f32[1,32]{1,0:T(1,128)}) custom-call(f32[1,32,1024]{2,1,0:T(8,128)} %get-tuple-element.10.refs_0_, f32[1,32]{1,0:T(1,128)} %get-tuple-element.11.refs_1_, f32[1,32,1024]{2,1,0:T(8,128)} %get-tuple-element.12.refs_2_, ...), custom_call_target="tpu_custom_call" | custom-call | tf_op jit(solution)/shard_map/pallas_call | solution.py:688
